TPU v7x, 256 devices: a whole 4x4x8 slice. The times are simulated.
256 devices in a mesh: gen: 8 (over z_lo, core), user: 16 (over x, y), cand: 2 (over z_hi).
Axes of the slice: x: 4, y: 4, z: 8 (z_hi: 2, z_lo: 4; z = z_hi * 4 + z_lo), core: 2. Of those that a mesh axis runs over, the one named last changes fastest.
Arguments:
- states: bfloat16 [16384, 4096], P(('user', 'cand')), may hold values from -6 to 6
- norm_gain: float32 [4096], replicated, may hold values from 0.1 to 1.9
- gate_weight: bfloat16 [4096, 7168], P('user', 'gen'), may hold values from -0.09375 to 0.09375
- up_weight: bfloat16 [4096, 7168], P('user', 'gen'), may hold values from -0.09375 to 0.09375
- down_weight: bfloat16 [7168, 4096], P('gen', 'user'), may hold values from -0.0625 to 0.0625
- proj_weight: bfloat16 [4096, 1024], P('gen'), may hold values from -0.09375 to 0.09375
- private_rows: bfloat16 [32768, 1024], P(('gen', 'user')), may hold values from -6 to 6
- enc_weight: bfloat16 [1024, 1024], replicated, may hold values from -0.1875 to 0.1875
- user_ids: int32 [32768], P(('gen', 'user')), may hold values from 0 to 31
Outputs:
- votes: float32 [16, 2, 128], P(None, 'cand')
Inputs may be any that keep to these rules, and one draw needn't show every extreme that they name: `user_ids`: a user is a pair of a block of 256 rows and a slot; no user has rows in two blocks.
All inputs are finite; a program needn't handle non-finite values.
Results may differ from a plain program's by a relative error of at most 0.0025.
Values may be sent and summed in bfloat16 or wider, within the bound.
No kernel may reach another device: no remote copies, remote signals or barrier semaphores. Data moves between devices by JAX's collectives and lax.ppermute only.
A program may use at most 128 MiB of HBM per device.

v0:
```python
import functools

import functools

import jax
import jax.numpy as jnp
from jax import lax
from jax.experimental import pallas as pl
from jax.experimental.pallas import tpu as pltpu
from jax.sharding import Mesh, PartitionSpec as P

STEPS = 4
CAP = 8
F32 = jnp.float32
BF16 = jnp.bfloat16
VMEM = pl.BlockSpec(memory_space=pltpu.VMEM)
ANY = pl.BlockSpec(memory_space=pl.ANY)


def z_pairs(pairs):
    place = lambda z: (z % 4) * 2 + z // 4
    return [(place(a % 8), place(b % 8)) for a, b in pairs]


def shift_z(a, k):
    return lax.ppermute(a, ("zl", "zh"), z_pairs([(z, z + k) for z in range(8)]))


def send_z(a, pairs):
    return lax.ppermute(a, ("zl", "zh"), z_pairs(pairs))


def shift(a, axis, k):
    return lax.ppermute(a, axis, [(i, (i + k) % 4) for i in range(4)])


def swap_core(a):
    return lax.ppermute(a, "core", [(0, 1), (1, 0)])


def pack_kernel(gate, up, down, gain, states, out_a, out_b, piece, sem):
    c, zl, core = lax.axis_index("zh"), lax.axis_index("zl"), lax.axis_index("core")
    user = lax.axis_index("x") * 4 + lax.axis_index("y")
    start = pl.multiple_of((3 - zl) * 128 + core * 64, 64)
    copy = pltpu.make_async_copy(states.at[pl.ds(start, 64)], piece, sem)
    copy.start()
    full = pl.ds(pl.multiple_of(c * 512, 128), 384)
    lane = lax.broadcasted_iota(jnp.int32, (128, 128), 1)
    for i, out in enumerate((out_a, out_b)):
        at = slice(i * 128, (i + 1) * 128)
        scale = jnp.broadcast_to(gain[pl.ds(user * 2 + i, 1), :], (128, 128)).T
        wide = jnp.concatenate([scale] * 3, 1)
        out[0:128, 0:384] = (gate[at, full].astype(F32) * wide).astype(BF16)
        out[0:128, 384:768] = (up[at, full].astype(F32) * wide).astype(BF16)
        g = gate[at, 384:512].astype(F32)
        u = up[at, 384:512].astype(F32)
        g = jnp.where(c == 0, g, pltpu.roll(g, 64, 1))
        u = jnp.where(c == 0, pltpu.roll(u, 64, 1), u)
        out[0:128, 768:896] = (jnp.where(lane < 64, g, u) * scale).astype(BF16)
        for j in range(7):
            first = 384 + c * 64 if j == 6 else c * 512 + j * 64
            rows = pl.ds(pl.multiple_of(first, 64), 64)
            out[128:192, j * 128 : (j + 1) * 128] = down[rows, at]
    copy.wait()


def pack_weights(gate, up, down, gain, states):
    d = states.shape[1]
    return pl.pallas_call(
        pack_kernel,
        out_shape=(jax.ShapeDtypeStruct((192, 896), BF16),) * 2 + (jax.ShapeDtypeStruct((64, d), BF16),),
        in_specs=[VMEM] * 4 + [ANY],
        out_specs=(VMEM,) * 3,
        scratch_shapes=[pltpu.SemaphoreType.DMA],
        name="pack_weights",
    )(gate, up, down, gain.reshape(d // 128, 128), states)


def run_copies(copies):
    for copy in copies:
        copy.start()
    for copy in copies:
        copy.wait()


def stack_kernel(groups, *refs):
    n = sum(groups)
    ins, outs, sems = refs[:n], refs[n:-1], refs[-1]
    copies, at = [], 0
    for size, out in zip(groups, outs):
        for k in range(size):
            copies.append(pltpu.make_async_copy(ins[at], out.at[k], sems.at[at]))
            at += 1
    run_copies(copies)


def stacks(*groups):
    arrays = [a for group in groups for a in group]
    out = tuple(jax.ShapeDtypeStruct((len(g),) + g[0].shape, g[0].dtype) for g in groups)
    return pl.pallas_call(
        functools.partial(stack_kernel, tuple(len(g) for g in groups)),
        out_shape=out,
        in_specs=[ANY] * len(arrays),
        out_specs=(VMEM,) * len(groups),
        scratch_shapes=[pltpu.SemaphoreType.DMA((len(arrays),))],
        name="stacks",
    )(*arrays)


def spread_first(chunk, axis):
    got = []
    for k in (-1, 2, 1):
        got.append(shift(chunk, axis, k))
    return got


def relay_kernel(states, q, *refs):
    outs, sems = refs[:4], refs[4]
    zl, core = lax.axis_index("zl"), lax.axis_index("core")
    for i, (out, end, piece) in enumerate(zip(outs, (3, 0, 3, 0), (2, 1, 3, 0))):
        own = states.at[pl.ds(pl.multiple_of(piece * 128 + core * 64, 64), 64)]
        pl.when(zl == end)(pltpu.make_async_copy(own, out, sems.at[i]).start)
        pl.when(zl != end)(pltpu.make_async_copy(q, out, sems.at[i]).start)
    for i, out in enumerate(outs):
        pltpu.make_async_copy(q, out, sems.at[i]).wait()


def join_kernel(q, p1, p2, p3, p4, out, sems):
    zl = lax.axis_index("zl")
    for i, p in enumerate((q, p1, p2)):
        pltpu.make_async_copy(p, out.at[pl.ds(i * 64, 64)], sems.at[i]).start()
    to = out.at[pl.ds(192, 64)]
    even = lax.rem(zl, 2) == 0
    pl.when(even)(pltpu.make_async_copy(p3, to, sems.at[3]).start)
    pl.when(jnp.logical_not(even))(pltpu.make_async_copy(p4, to, sems.at[3]).start)
    for i in range(4):
        pltpu.make_async_copy(q, out.at[pl.ds(i * 64, 64)], sems.at[i]).wait()


def exchange_states(states, q):
    sent = jax.ShapeDtypeStruct(q.shape, q.dtype)
    up, dn, up2, dn2 = pl.pallas_call(
        relay_kernel,
        out_shape=(sent,) * 4,
        in_specs=[ANY] * 2,
        out_specs=(VMEM,) * 4,
        scratch_shapes=[pltpu.SemaphoreType.DMA((4,))],
        name="relay",
    )(states, q)
    p1 = shift_z(up, 1)
    p2 = shift_z(dn, -1)
    p3 = send_z(up2, [(0, 2), (4, 6), (3, 4), (7, 0)])
    p4 = send_z(dn2, [(3, 1), (7, 5), (0, 7), (4, 3)])
    return pl.pallas_call(
        join_kernel,
        out_shape=jax.ShapeDtypeStruct((256, q.shape[1]), q.dtype),
        in_specs=[ANY] * 5,
        out_specs=VMEM,
        scratch_shapes=[pltpu.SemaphoreType.DMA((4,))],
        name="join",
    )(q, p1, p2, p3, p4)


def places():
    zl, core, c = lax.axis_index("zl"), lax.axis_index("core"), lax.axis_index("zh")
    pieces = (
        zl,
        jnp.where(zl == 0, 2, zl - 1),
        jnp.where(zl == 3, 1, zl + 1),
        jnp.where(zl < 2, 3, 0),
    )
    own = [c * 8 + i for i in range(8)]
    part = [(1 - c) * 8 + p * 2 + core for p in pieces]
    other = [(1 - c) * 8 + p * 2 + 1 - core for p in pieces]
    return own + part + other


def user_of(colour, m, k):
    x, y = lax.axis_index("x"), lax.axis_index("y")
    if isinstance(colour, int):
        dx, dy = (k, m) if colour == 0 else (m, k)
    else:
        dx, dy = jnp.where(colour == 0, k, m), jnp.where(colour == 0, m, k)
    return lax.rem(x + dx, 4), lax.rem(y + dy, 4)


def ff_kernel(own, part, other, *refs):
    n = 4 * len(ORDER)
    bundles, refs = refs[:n], refs[n:]
    hp_ref, tok, acc, squares, held, sems = refs
    copies = [
        pltpu.make_async_copy(b.at[:, pl.ds(0, 128)], held.at[i // 2, pl.ds(i % 2 * 2, 2)], sems.at[i])
        for i, b in enumerate(bundles)
    ]
    toks = [
        pltpu.make_async_copy(own, tok.at[0], sems.at[n]),
        pltpu.make_async_copy(part, tok.at[1, pl.ds(0, 256)], sems.at[n + 1]),
        pltpu.make_async_copy(other, tok.at[1, pl.ds(256, 256)], sems.at[n + 2]),
    ]
    toks[0].start()
    for copy in copies + toks[1:]:
        copy.start()
    place = places()
    row = lax.broadcasted_iota(jnp.int32, (64, 256), 0)
    col = lax.broadcasted_iota(jnp.int32, (64, 256), 1)
    pool = (col // STEPS == row).astype(BF16)
    lane = lax.broadcasted_iota(jnp.int32, (256, 128), 1)

    def rows(i, _):
        pl.when(i == 0)(toks[0].wait)
        pl.when(i == 1)(toks[1].wait)
        pl.when(i == 1)(toks[2].wait)
        squares[...] = jnp.zeros_like(squares)

        def colours(colour, _):
            for b, m in enumerate(ORDER):
                for c in range(2):
                    for h in range(2):
                        due = jnp.logical_and(i == 0, colour == c)
                        pl.when(due)(copies[2 * (4 * c + b) + h].wait)
                xs, ws, square = [], [], None
                for k in range(4):
                    ux, uy = user_of(colour, m, k)
                    at = pl.multiple_of((ux * 4 + uy) * 256 + colour * 128, 128)
                    x = tok[i, :, pl.ds(at, 128)]
                    wide = x.astype(F32)
                    square = wide * wide if square is None else square + wide * wide
                    xs.append(x)
                    ws.append(held[4 * colour + b, k])
                squares[...] += square
                d = jnp.dot(jnp.concatenate(xs, 1), jnp.concatenate(ws, 0), preferred_element_type=F32)
                if b == 0:
                    acc[...] = d + jnp.where(colour == 0, 0.0, acc[...])
                else:
                    acc[...] += d
            return 0

        lax.fori_loop(0, 2, colours, 0)
        scale = lax.rsqrt(jnp.sum(squares[...], axis=1, keepdims=True) / tok.shape[2] + 1e-05)
        for j in range(2):
            at = slice(j * 256, (j + 1) * 256)
            gate = acc[at, 0:384] * scale[at]
            up = acc[at, 384:768] * scale[at]
            mixed = acc[at, 768:896] * scale[at]
            hidden = (jax.nn.silu(gate) * up).astype(BF16)
            rest = jnp.where(lane < 64, jax.nn.silu(mixed) * pltpu.roll(mixed, 64, 1), 0.0).astype(BF16)
            hp = jnp.dot(pool, hidden, preferred_element_type=F32).astype(BF16)
            hp_rest = jnp.dot(pool, rest, preferred_element_type=F32).astype(BF16)
            for t in range(4):
                to = jnp.where(i == 0, place[j * 4 + t], place[8 + j * 4 + t])
                to = pl.ds(pl.multiple_of(to * 16, 16), 16)
                hp_ref[to, 0:384] = hp[t * 16 : (t + 1) * 16]
                hp_ref[to, 384:512] = hp_rest[t * 16 : (t + 1) * 16]
        return 0

    lax.fori_loop(0, 2, rows, 0)


def feed_forward(own, part, other, bundles):
    args = (own, part, other, *bundles)
    return pl.pallas_call(
        ff_kernel,
        out_shape=jax.ShapeDtypeStruct((256, 512), BF16),
        in_specs=[ANY] * len(args),
        out_specs=VMEM,
        scratch_shapes=[
            pltpu.VMEM((2, 512, own.shape[1]), BF16),
            pltpu.VMEM((512, 896), F32),
            pltpu.VMEM((512, 128), F32),
            pltpu.VMEM((2 * len(ORDER), 4, 128, 896), BF16),
            pltpu.SemaphoreType.DMA((4 * len(ORDER) + 3,)),
        ],
        name="feed_forward",
    )(*args)


def w2_kernel(spec, mine, theirs, *refs):
    bundles, out = refs[:-1], refs[-1]
    zl, core = lax.axis_index("zl"), lax.axis_index("core")
    acc = None
    for b, (colour, m) in enumerate(spec):
        ds, ps = [], []
        for k in range(4):
            ux, uy = user_of(colour, m, k)
            ds.append(jnp.concatenate([bundles[2 * b + k // 2][k % 2, :, j * 128 : (j + 1) * 128] for j in range(7)], 0))
            rel = lax.rem(ux - zl + 4, 4)
            col = pl.ds(pl.multiple_of((lax.rem(uy, 2) * 2 + colour) * 256, 256), 256)
            ps.append(jnp.where(uy // 2 == core, mine[rel, :, col], theirs[rel, :, col]))
        d = jnp.dot(jnp.concatenate(ds, 1), jnp.concatenate(ps, 0), preferred_element_type=F32)
        acc = d if acc is None else acc + d
    out[0:448, :] = acc.astype(BF16)
    out[448:512, :] = jnp.zeros((64, 256), BF16)


def down_proj(spec, mine, theirs, bundles):
    whole = pl.BlockSpec((4, 128, 1024), lambda i: (0, 0, 0))
    return pl.pallas_call(
        functools.partial(w2_kernel, spec),
        out_shape=jax.ShapeDtypeStruct((512, 256), BF16),
        grid=(1,),
        in_specs=[whole, whole] + [pl.BlockSpec((b.shape[0], 64, 896), lambda i: (0, 2, 0)) for b in bundles],
        out_specs=pl.BlockSpec((512, 256), lambda i: (0, 0)),
        name="down_proj",
    )(mine, theirs, *bundles)


def embed_kernel(hp, w0, w1, w2, w3, resid, keep, send, emb):
    y, core, zh = lax.axis_index("y"), lax.axis_index("core"), lax.axis_index("zh")
    for k, w in enumerate((w0, w1, w2, w3)):
        col = pl.ds(pl.multiple_of(lax.rem(y + k, 4) * 256, 256), 256)
        emb[:, col] = jnp.dot(hp[...], w[...], preferred_element_type=F32)
    half = pl.ds(pl.multiple_of(zh * 128, 128), 128)
    emb[half, :] += resid[...]
    for z in range(4):
        for c in range(2):
            at = pl.ds((z * 2 + c) * 16, 16)
            base = c * 128 + z * 32
            keep[at, :] = emb[pl.ds(pl.multiple_of(base + core * 16, 16), 16), :] * (1.0 / STEPS)
            send[at, :] = emb[pl.ds(pl.multiple_of(base + 16 - core * 16, 16), 16), :] * (1.0 / STEPS)


def embed(hp, parts, resid):
    shape = jax.ShapeDtypeStruct((128, 1024), F32)
    return pl.pallas_call(
        embed_kernel,
        out_shape=(shape, shape),
        in_specs=[VMEM] * 6,
        out_specs=(VMEM, VMEM),
        scratch_shapes=[pltpu.VMEM((256, 1024), F32)],
        name="embed",
    )(hp, *parts, resid)


def unit_rows(matrix):
    return (matrix * lax.rsqrt(jnp.sum(matrix * matrix, axis=1, keepdims=True) + 1e-06)).astype(BF16)


def candidate_kernel(parts, out):
    total = parts[0].astype(F32)
    for i in range(1, 8):
        total += parts[i].astype(F32)
    cand = unit_rows(total)
    for i in range(16):
        out[i] = cand


def candidates(parts):
    return pl.pallas_call(
        candidate_kernel,
        out_shape=jax.ShapeDtypeStruct((16, 16, 1024), BF16),
        in_specs=[VMEM],
        out_specs=VMEM,
        name="candidates",
    )(parts)


def row_of(k, s):
    core = lax.axis_index("core")
    core = core if s == 0 else 1 - core
    return lax.rem(lax.axis_index("zl") + k, 4) * 2 + core


def score_kernel(cands, mine, theirs, ids_row, ids_col, kernel_ref, note_ref, note):
    match = (ids_row[...] == ids_col[...]).astype(F32)
    count = jnp.sum(match, axis=0, keepdims=True)
    note[8:16, :] = jnp.broadcast_to(jnp.minimum(1.0, CAP / count), (8, 256))

    def block(k, _):
        for s, rows in enumerate((mine, theirs)):
            scores = lax.dot_general(
                cands[...], rows[k], (((1,), (1,)), ((), ())), preferred_element_type=F32
            )
            kernel = jnp.exp(scores * 60.0)
            kernel_ref[:, pl.ds(pl.multiple_of(s * 1024 + k * 256, 256), 256)] = kernel
            note[pl.ds(row_of(k, s), 1), :] = jnp.sum(kernel, axis=0, keepdims=True)
        return 0

    lax.fori_loop(0, 4, block, 0)
    for i in range(16):
        note_ref[i] = note[...]


def score(cands, mine, theirs, ids):
    return pl.pallas_call(
        score_kernel,
        out_shape=(
            jax.ShapeDtypeStruct((256, 2048), F32),
            jax.ShapeDtypeStruct((16, 16, 256), F32),
        ),
        in_specs=[VMEM] * 5,
        out_specs=(VMEM, VMEM),
        scratch_shapes=[pltpu.VMEM((16, 256), F32)],
        name="score",
    )(cands, mine, theirs, ids.reshape(1, 256), ids.reshape(256, 1))


def vote_kernel(notes, kernel, out, weight):
    totals = notes[0, 0:8, :]
    for i in range(1, 16):
        totals += notes[i, 0:8, :]
    for r in range(8):
        weight[r : r + 1, :] = notes[2 * r, 8:9, :] / totals[r : r + 1] * (4096 / 32768)
    acc = None
    for b in range(8):
        w = weight[pl.ds(row_of(b % 4, b // 4), 1), :]
        part = kernel[:, b * 256 : (b + 1) * 256] * w
        acc = part if acc is None else acc + part
    votes = jnp.sum(acc.T, axis=0, keepdims=True)
    pair = jnp.concatenate([votes[:, :128], votes[:, 128:]], 0)
    out[...] = jnp.broadcast_to(pair[None], (128, 2, 128))


def vote(notes, kernel):
    return pl.pallas_call(
        vote_kernel,
        out_shape=jax.ShapeDtypeStruct((128, 2, 128), F32),
        in_specs=[VMEM, VMEM],
        out_specs=VMEM,
        scratch_shapes=[pltpu.VMEM((8, 256), F32)],
        name="vote",
    )(notes, kernel)


def final_kernel(parts, out):
    lane = lax.broadcasted_iota(jnp.int32, (2, 128), 1)
    for g in range(8):
        total = parts[g * 16]
        for i in range(1, 16):
            total += parts[g * 16 + i]
        for r in range(8):
            moved = pltpu.roll(total, (g * 16 - r * 16) % 128, 1)
            here = jnp.logical_and(lane >= g * 16, lane < g * 16 + 16)
            old = out[:, r, :] if g > 0 else jnp.zeros((2, 128), F32)
            out[:, r, :] = jnp.where(here, moved, old)


def gather_votes(parts):
    return pl.pallas_call(
        final_kernel,
        out_shape=jax.ShapeDtypeStruct((2, 8, 128), F32),
        in_specs=[VMEM],
        out_specs=VMEM,
        name="gather_votes",
    )(parts)


ORDER = (0, 1, 3, 2)
BUNDLES = tuple((colour, m) for colour in range(2) for m in ORDER)


def shards(states, norm_gain, gate, up, down, proj, rows, enc, ids):
    zl, core, y = lax.axis_index("zl"), lax.axis_index("core"), lax.axis_index("y")
    a, b, piece = pack_weights(gate, up, down, norm_gain, states)
    q = send_z(piece, [(z, 7 - z) for z in range(8)])
    near_a = spread_first(a, "x")
    near_b = spread_first(b, "y")
    cols = lax.dynamic_slice_in_dim(proj, y * 256, 256, 1)
    cols = jnp.concatenate([cols[i * 128 : (i + 1) * 128] for i in range(4)], axis=1)
    near_cols = []
    for k in (-1, 2, 1):
        near_cols.append(shift_z(cols, k))
    a_lo, a_hi, b_lo, b_hi = stacks((a, near_a[0]), near_a[1:], (b, near_b[0]), near_b[1:])
    moves = [(a_lo, "y", 1), (a_hi, "y", -1), (b_lo, "x", 1), (b_hi, "x", -1)]
    moves += [(a_hi, "y", 1), (a_lo, "y", -1), (b_hi, "x", 1), (b_lo, "x", -1)]
    got = []
    for bundle, axis, k in moves:
        got.append(shift(bundle, axis, k))
    near = (a_lo, a_hi, got[5], got[1], got[0], got[4], b_lo, b_hi, got[7], got[3], got[2], got[6])
    part = exchange_states(states, q)
    pool = (jnp.arange(512)[None, :] // STEPS == jnp.arange(128)[:, None]).astype(BF16)
    state_cols = lax.dynamic_slice_in_dim(states, (zl * 2 + core) * 512, 512, 1)
    resid = jnp.dot(pool, state_cols, preferred_element_type=F32).astype(BF16)
    resid = jnp.dot(resid, proj, preferred_element_type=F32)
    encoded = unit_rows(jnp.dot(rows, enc, preferred_element_type=F32))
    (cols,) = stacks((cols, *near_cols))
    cols_other = swap_core(cols)
    far = []
    for i, (_, axis, k) in enumerate(moves[:4]):
        far.append(shift(got[i], axis, k))
    part, resid, encoded = lax.optimization_barrier((part, resid, encoded))
    other = swap_core(part)
    near_rows = []
    for k in (-1, 2, 1):
        near_rows.append(shift_z(encoded, k))
    bundles = near[:6] + tuple(far[:2]) + near[6:] + tuple(far[2:])
    w2 = down_proj(BUNDLES, cols, cols_other, bundles)
    parts = [w2]
    for k in (-1, 2, 1):
        parts.append(shift(w2, "y", k))
    hp = feed_forward(states, part, other, bundles)
    keep, send = embed(hp, parts, resid)
    emb = (keep + swap_core(send)).astype(BF16).reshape(8, 16, 1024)
    emb = lax.all_to_all(emb, ("zl", "zh"), 0, 0)
    cands, near = lax.optimization_barrier((candidates(emb), near_rows))
    (encoded,) = stacks((encoded, *near_rows))
    encoded_other = swap_core(encoded)
    cands = lax.all_to_all(cands, ("x", "y"), 0, 0).reshape(256, 1024)
    kernel, note = score(cands, encoded, encoded_other, ids)
    notes = lax.all_to_all(note, ("zl", "core", "zh"), 0, 0)
    partial = lax.all_to_all(vote(notes, kernel), ("zl", "core", "x", "y"), 0, 0)
    return gather_votes(partial).reshape(16, 1, 128)


def solution(mesh):
    fine = Mesh(mesh.devices.reshape(4, 2, 4, 4, 2), ("zl", "core", "x", "y", "zh"))
    gen, user, cand = ("zl", "core"), ("x", "y"), "zh"

    return jax.shard_map(
        shards,
        mesh=fine,
        in_specs=(
            P(user + (cand,), None),
            P(),
            P(user, gen),
            P(user, gen),
            P(gen, user),
            P(gen, None),
            P(gen + user, None),
            P(),
            P(gen + user),
        ),
        out_specs=P(None, cand, None),
        check_vma=False,
    )
```

profile of v0, /device:TPU:0, one launch (start us, length us, event | category | flops | bytes accessed | tf_op | source)
XLA Modules:
  0.0 280.5 jit_solution(6868296873840047805)
XLA Ops:
  0.0 3.7 %pack_weights.1 = (bf16[192,896]{1,0:T(8,128)(2,1)}, bf16[192,896]{1,0:T(8,128)(2,1)}, bf16[64,4096]{1,0:T(8,128)(2,1)}) custom-call(bf16[256,896]{1,0:T(8,128)(2,1)} %gate.1, bf16[256,896]{1,0:T(8,128)(2,1)} %up.1, bf16[896,256]{1,0:T(8,128)(2,1)} %down.1, f32[32,128]{1,0:T(8,128)} %bitcast.13, bf16[512,4096]{1,0:T(8,128)(2,1)} %own.1), custom_call_target="tpu_custom_call" | custom-call | tf_op jit(solution)/shard_map/pack_weights/pallas_call | solution.py:69
  3.7 1.1 collective-permute-start.6
  4.8 0.8 collective-permute-start.7
  5.6 0.9 collective-permute-start.8
  6.5 3.0 %collective-permute-start.9 = (bf16[192,896]{1,0:T(8,128)(2,1)}, bf16[192,896]{1,0:T(8,128)(2,1)}, u32[]{:S(2)}, u32[]{:S(2)}) collective-permute-start(bf16[192,896]{1,0:T(8,128)(2,1)} %get-tuple-element.31.refs_4_), channel_id=1, source_target_pairs={{0,6},{2,0},{4,2},{6,4},{1,7},{3,1},{5,3},{7,5},{8,14},{10,8},{12,... | collective-permute-start | bytes 1032200 | tf_op jit(solution)/shard_map/ppermute | solution.py:34
  9.5 0.6 collective-permute-start.10
  10.1 1.0 constant_dynamic-slice_fusion
  11.1 8.7 %collective-permute-done.6.refs_1_ = bf16[192,896]{1,0:T(8,128)(2,1)S(1)} collective-permute-done((bf16[192,896]{1,0:T(8,128)(2,1)}, bf16[192,896]{1,0:T(8,128)(2,1)S(1)}, u32[]{:S(2)}, u32[]{:S(2)}) %collective-permute-start.6) | collective-permute-done | bytes 344096 | tf_op jit(solution)/shard_map/ppermute | solution.py:34
  19.8 1.6 collective-permute-start.11
  21.5 5.9 %collective-permute-start.24 = (bf16[128,1024]{1,0:T(8,128)(2,1)S(1)}, bf16[128,1024]{1,0:T(8,128)(2,1)}, u32[]{:S(2)}, u32[]{:S(2)}) collective-permute-start(bf16[128,1024]{1,0:T(8,128)(2,1)S(1)} %pad_maximum_fusion.refs_0_), channel_id=1, source_target_pairs={{0,193},{64,0},{128,64},{192,128},{1,192},{65,1},{129,65},{193,129... | collective-permute-start | bytes 786440 | tf_op jit(solution)/shard_map/ppermute | solution.py:26
  27.4 2.1 collective-permute-start
  29.5 3.4 %stacks.3 = (bf16[2,192,896]{2,1,0:T(8,128)(2,1)}, bf16[2,192,896]{2,1,0:T(8,128)(2,1)}, bf16[2,192,896]{2,1,0:T(8,128)(2,1)}, bf16[2,192,896]{2,1,0:T(8,128)(2,1)}) custom-call(bf16[192,896]{1,0:T(8,128)(2,1)} %get-tuple-element.30.refs_0_, bf16[192,896]{1,0:T(8,128)(2,1)} %copy-done.6, bf16[192,896]{1,0:T(8,128)(2,1)} %copy-done.7, ...), custom_call_target="tpu_custom_call" | custom-call | tf_op jit(solution)/shard_map/stacks/pallas_call | solution.py:100
  33.0 3.8 %collective-permute-start.12 = (bf16[2,192,896]{2,1,0:T(8,128)(2,1)}, bf16[2,192,896]{2,1,0:T(8,128)(2,1)}, u32[]{:S(2)}, u32[]{:S(2)}) collective-permute-start(bf16[2,192,896]{2,1,0:T(8,128)(2,1)} %get-tuple-element.32.refs_0_), channel_id=1, source_target_pairs={{0,6},{2,0},{4,2},{6,4},{1,7},{3,1},{5,3},{7,5},{8,14},{10,8},{12,... | collective-permute-start | bytes 2064392 | tf_op jit(solution)/shard_map/ppermute | solution.py:34
  36.8 7.2 %collective-permute-done.24.refs_1_ = bf16[128,1024]{1,0:T(8,128)(2,1)} collective-permute-done((bf16[128,1024]{1,0:T(8,128)(2,1)S(1)}, bf16[128,1024]{1,0:T(8,128)(2,1)}, u32[]{:S(2)}, u32[]{:S(2)}) %collective-permute-start.24) | collective-permute-done | bytes 262176 | tf_op jit(solution)/shard_map/ppermute | solution.py:26
  44.0 1.6 collective-permute-start.14
  45.6 0.8 collective-permute-start.15
  46.5 17.5 %collective-permute-done.q = bf16[64,4096]{1,0:T(8,128)(2,1)S(1)} collective-permute-done((bf16[64,4096]{1,0:T(8,128)(2,1)}, bf16[64,4096]{1,0:T(8,128)(2,1)S(1)}, u32[]{:S(2)}, u32[]{:S(2)}) %collective-permute-start) | collective-permute-done | bytes 524320 | tf_op jit(solution)/shard_map/ppermute | solution.py:30
  63.9 0.8 copy-done.3
  64.7 1.8 multiply_reduce_fusion
  66.6 2.9 %relay.1 = (bf16[64,4096]{1,0:T(8,128)(2,1)}, bf16[64,4096]{1,0:T(8,128)(2,1)}, bf16[64,4096]{1,0:T(8,128)(2,1)}, bf16[64,4096]{1,0:T(8,128)(2,1)}) custom-call(bf16[512,4096]{1,0:T(8,128)(2,1)} %own.1, bf16[64,4096]{1,0:T(8,128)(2,1)} %copy-done.3), custom_call_target="tpu_custom_call" | custom-call | tf_op jit(solution)/shard_map/relay/pallas_call | solution.py:142
  69.5 4.4 %collective-permute-done.26.refs_3_ = bf16[128,1024]{1,0:T(8,128)(2,1)} collective-permute-done((bf16[128,1024]{1,0:T(8,128)(2,1)S(1)}, bf16[128,1024]{1,0:T(8,128)(2,1)}, u32[]{:S(2)}, u32[]{:S(2)}) %collective-permute-start.26) | collective-permute-done | bytes 262176 | tf_op jit(solution)/shard_map/ppermute | solution.py:26
  74.0 3.2 %collective-permute-start.2 = (bf16[64,4096]{1,0:T(8,128)(2,1)}, bf16[64,4096]{1,0:T(8,128)(2,1)}, u32[]{:S(2)}, u32[]{:S(2)}) collective-permute-start(bf16[64,4096]{1,0:T(8,128)(2,1)} %get-tuple-element.26), channel_id=1, source_target_pairs={{0,193},{64,0},{128,64},{192,128},{1,192},{65,1},{129,65},{193,129... | collective-permute-start | bytes 1572872 | tf_op jit(solution)/shard_map/ppermute | solution.py:26
  77.2 1.9 collective-permute-start.3
  79.1 6.8 %collective-permute-start.4 = (bf16[64,4096]{1,0:T(8,128)(2,1)}, bf16[64,4096]{1,0:T(8,128)(2,1)}, u32[]{:S(2)}, u32[]{:S(2)}) collective-permute-start(bf16[64,4096]{1,0:T(8,128)(2,1)} %get-tuple-element.28), channel_id=1, source_target_pairs={{192,64},{193,65},{0,193},{1,192},{194,66},{195,67},{2,195},{3,194... | collective-permute-start | bytes 1572872 | tf_op jit(solution)/shard_map/ppermute | solution.py:30
  85.9 2.7 fusion.resid
  88.6 2.2 stacks.4.mine
  90.9 2.1 collective-permute-start.20
  93.0 6.4 %collective-permute-done.3.p3 = bf16[64,4096]{1,0:T(8,128)(2,1)} collective-permute-done((bf16[64,4096]{1,0:T(8,128)(2,1)}, bf16[64,4096]{1,0:T(8,128)(2,1)}, u32[]{:S(2)}, u32[]{:S(2)}) %collective-permute-start.3) | collective-permute-done | bytes 524320 | tf_op jit(solution)/shard_map/ppermute | solution.py:30
  99.4 1.1 collective-permute-start.19
  100.4 0.9 collective-permute-start.21
  101.4 0.9 multiply_convert_fusion.refs_0_
  102.3 2.9 %join.1.part = bf16[256,4096]{1,0:T(8,128)(2,1)} custom-call(bf16[64,4096]{1,0:T(8,128)(2,1)} %copy-done.3, bf16[64,4096]{1,0:T(8,128)(2,1)} %collective-permute-done.1.p1, bf16[64,4096]{1,0:T(8,128)(2,1)} %collective-permute-done.2.p2, bf16[64,4096]{1,0:T(8,128)(2,1)} %collective-permute-done.3.p3, bf16[64,4096]{1,0:T(8,128)(2,1)} %collective-permute-done.4.p4), custom_call_target="tpu_custom_call" | custom-call | tf_op jit(solution)/shard_map/join/pallas_call | solution.py:154
  105.3 9.7 %collective-permute-done.19.refs_11_ = bf16[2,192,896]{2,1,0:T(8,128)(2,1)} collective-permute-done((bf16[2,192,896]{2,1,0:T(8,128)(2,1)}, bf16[2,192,896]{2,1,0:T(8,128)(2,1)}, u32[]{:S(2)}, u32[]{:S(2)}) %collective-permute-start.19) | collective-permute-done | bytes 688160 | tf_op jit(solution)/shard_map/ppermute | solution.py:34
  115.0 0.3 collective-permute-start.33
  115.2 9.8 %collective-permute-done.21.refs_13_ = bf16[2,192,896]{2,1,0:T(8,128)(2,1)} collective-permute-done((bf16[2,192,896]{2,1,0:T(8,128)(2,1)}, bf16[2,192,896]{2,1,0:T(8,128)(2,1)}, u32[]{:S(2)}, u32[]{:S(2)}) %collective-permute-start.21) | collective-permute-done | bytes 688160 | tf_op jit(solution)/shard_map/ppermute | solution.py:34
  125.0 1.5 collective-permute-start.16
  126.5 2.8 collective-permute-start.17
  129.2 14.1 %collective-permute-done.33.refs_2_ = bf16[256,1024]{1,0:T(8,128)(2,1)} collective-permute-done((bf16[256,1024]{1,0:T(8,128)(2,1)}, bf16[256,1024]{1,0:T(8,128)(2,1)}, u32[]{:S(2)}, u32[]{:S(2)}) %collective-permute-start.33) | collective-permute-done | bytes 524320 | tf_op jit(solution)/shard_map/ppermute | solution.py:26
  143.3 1.5 collective-permute-start.22
  144.8 6.0 %collective-permute-done.34.refs_3_ = bf16[256,1024]{1,0:T(8,128)(2,1)} collective-permute-done((bf16[256,1024]{1,0:T(8,128)(2,1)}, bf16[256,1024]{1,0:T(8,128)(2,1)}, u32[]{:S(2)}, u32[]{:S(2)}) %collective-permute-start.34) | collective-permute-done | bytes 524320 | tf_op jit(solution)/shard_map/ppermute | solution.py:26
  150.8 1.7 collective-permute-start.23
  152.5 2.9 %stacks.5.mine = bf16[4,256,1024]{2,1,0:T(8,128)(2,1)} custom-call(bf16[256,1024]{1,0:T(8,128)(2,1)} %multiply_convert_fusion.refs_0_, bf16[256,1024]{1,0:T(8,128)(2,1)} %collective-permute-done.32.refs_1_, bf16[256,1024]{1,0:T(8,128)(2,1)} %collective-permute-done.33.refs_2_, bf16[256,1024]{1,0:T(8,128)(2,1)} %collective-permute-done.34.refs_3_), custom_call_target="tpu_custom_call" | custom-call | tf_op jit(solution)/shard_map/stacks/pallas_call | solution.py:100
  155.6 0.2 collective-permute-done.22.refs_14_
  155.8 12.7 %collective-permute-done.23.refs_15_ = bf16[2,192,896]{2,1,0:T(8,128)(2,1)} collective-permute-done((bf16[2,192,896]{2,1,0:T(8,128)(2,1)}, bf16[2,192,896]{2,1,0:T(8,128)(2,1)}, u32[]{:S(2)}, u32[]{:S(2)}) %collective-permute-start.23) | collective-permute-done | bytes 688160 | tf_op jit(solution)/shard_map/ppermute | solution.py:34
  168.5 4.5 %down_proj.1.w0 = bf16[512,256]{1,0:T(8,128)(2,1)} custom-call(bf16[4,128,1024]{2,1,0:T(8,128)(2,1)} %stacks.4.mine, bf16[4,128,1024]{2,1,0:T(8,128)(2,1)} %collective-permute-done.27.theirs, bf16[2,192,896]{2,1,0:T(8,128)(2,1)} %get-tuple-element.32.refs_0_, bf16[2,192,896]{2,1,0:T(8,128)(2,1)} %get-tuple-element.33.refs_1_, ...), custom_call_target="tpu_custom_call" | custom-call | tf_op jit(solution)/shard_map/down_proj/pallas_call | solution.py:297
  173.0 3.0 %collective-permute-start.28 = (bf16[512,256]{1,0:T(8,128)(2,1)}, bf16[512,256]{1,0:T(8,128)(2,1)S(1)}, u32[]{:S(2)}, u32[]{:S(2)}) collective-permute-start(bf16[512,256]{1,0:T(8,128)(2,1)} %down_proj.1.w0), channel_id=1, source_target_pairs={{0,6},{2,0},{4,2},{6,4},{1,7},{3,1},{5,3},{7,5},{8,14},{10,8},{12,... | collective-permute-start | bytes 786440 | tf_op jit(solution)/shard_map/ppermute | solution.py:34
  176.3 1.0 collective-permute-start.30
  177.2 15.5 %feed_forward.1.hp = bf16[256,512]{1,0:T(8,128)(2,1)} custom-call(bf16[512,4096]{1,0:T(8,128)(2,1)} %own.1, bf16[256,4096]{1,0:T(8,128)(2,1)} %join.1.part, bf16[256,4096]{1,0:T(8,128)(2,1)} %collective-permute-done.5.other, bf16[2,192,896]{2,1,0:T(8,128)(2,1)} %get-tuple-element.32.refs_0_, bf16[2,192,896]{2,1,0:T(8,128)(2,1)} %get-tuple-element.33.refs_1_, ...), custom_call_target="tpu_custom_call" | custom-call | tf_op jit(solution)/shard_map/feed_forward/pallas_call | solution.py:261
  192.8 0.7 copy-done.8
  193.6 0.7 copy-done.10
  194.3 3.0 %embed.1 = (f32[128,1024]{1,0:T(8,128)}, f32[128,1024]{1,0:T(8,128)}) custom-call(bf16[256,512]{1,0:T(8,128)(2,1)} %feed_forward.1.hp, bf16[512,256]{1,0:T(8,128)(2,1)} %down_proj.1.w0, bf16[512,256]{1,0:T(8,128)(2,1)} %copy-done.8, bf16[512,256]{1,0:T(8,128)(2,1)} %copy-done.9, bf16[512,256]{1,0:T(8,128)(2,1)} %copy-done.10, f32[128,1024]{1,0:T(8,128)} %fusion.resid), custom_call_target="tpu_custom_call" | custom-call | tf_op jit(solution)/shard_map/embed/pallas_call | solution.py:324
  197.3 2.1 collective-permute-done.31
  199.4 1.1 add_convert_fusion
  200.6 15.2 %all_to_all.20.parts = bf16[8,16,1024]{2,1,0:T(8,128)(2,1)} all-to-all(bf16[8,16,1024]{2,1,0:T(8,128)(2,1)S(1)} %bitcast.12), channel_id=1, replica_groups=mesh['zl'=4,'core'=2,'x'=4,'y'=4,'zh'=2] {'zl','zh'}, dimensions={0} | all-to-all | bytes 524288 | tf_op jit(solution)/shard_map/all_to_all | solution.py:493
  215.7 1.9 candidates.1
  217.6 6.1 %all-to-all-start.1 = ((bf16[16,16,1024]{2,1,0:T(8,128)(2,1)}), bf16[16,16,1024]{2,1,0:T(8,128)(2,1)S(1)}, u32[]{:S(2)}, u32[]{:S(2)}) async-start(bf16[16,16,1024]{2,1,0:T(8,128)(2,1)} %candidates.1), calls=%async_computation.1 | async-start | bytes 1048576 | tf_op jit(solution)/shard_map/all_to_all | solution.py:497
  223.7 0.8 copy.11.ids_col
  224.5 9.3 %all-to-all-done.1 = bf16[16,16,1024]{2,1,0:T(8,128)(2,1)S(1)} async-done(((bf16[16,16,1024]{2,1,0:T(8,128)(2,1)}), bf16[16,16,1024]{2,1,0:T(8,128)(2,1)S(1)}, u32[]{:S(2)}, u32[]{:S(2)}) %all-to-all-start.1) | async-done | bytes 524320 | tf_op jit(solution)/shard_map/all_to_all | solution.py:497
  233.8 0.8 copy-done.4
  234.6 5.9 %score.1 = (f32[256,2048]{1,0:T(8,128)}, f32[16,16,256]{2,1,0:T(8,128)}) custom-call(bf16[256,1024]{1,0:T(8,128)(2,1)} %bitcast.11, bf16[4,256,1024]{2,1,0:T(8,128)(2,1)} %stacks.5.mine, bf16[4,256,1024]{2,1,0:T(8,128)(2,1)} %collective-permute-done.35.theirs, s32[1,256]{1,0:T(1,128)} %bitcast.14, s32[256,1]{1,0:T(8,128)} %copy.11.ids_col), custom_call_target="tpu_custom_call" | custom-call | tf_op jit(solution)/shard_map/score/pallas_call | solution.py:384
  240.5 18.6 %all_to_all.21.notes = f32[16,16,256]{2,1,0:T(8,128)} all-to-all(f32[16,16,256]{2,1,0:T(8,128)} %get-tuple-element.41), channel_id=1, replica_groups=mesh['zl'=4,'core'=2,'x'=4,'y'=4,'zh'=2] {'zl','core','zh'}, dimensions={0} | all-to-all | bytes 524288 | tf_op jit(solution)/shard_map/all_to_all | solution.py:499
  259.1 2.6 vote.1
  261.7 17.1 %all_to_all.22.parts = f32[128,2,128]{2,1,0:T(2,128)} all-to-all(f32[128,2,128]{2,1,0:T(2,128)} %vote.1), channel_id=1, replica_groups=mesh['zl'=4,'core'=2,'x'=4,'y'=4,'zh'=2] {'zl','core','x','y'}, dimensions={0} | all-to-all | bytes 262144 | tf_op jit(solution)/shard_map/all_to_all | solution.py:500
  278.8 1.7 gather_votes.1
  (59 shorter events, 0.8 us)
Async XLA Ops:
  0.0 64.7 %copy-start = (bf16[1024,1024]{1,0:T(8,128)(2,1)S(1)}, bf16[1024,1024]{1,0:T(8,128)(2,1)}, u32[]{:S(2)}) copy-start(bf16[1024,1024]{1,0:T(8,128)(2,1)} %param.16) | copy-start | bytes 6291460
  3.7 16.1 %collective-permute-start.6 = (bf16[192,896]{1,0:T(8,128)(2,1)}, bf16[192,896]{1,0:T(8,128)(2,1)S(1)}, u32[]{:S(2)}, u32[]{:S(2)}) collective-permute-start(bf16[192,896]{1,0:T(8,128)(2,1)} %get-tuple-element.30.refs_0_), channel_id=1, source_target_pairs={{0,24},{8,0},{16,8},{24,16},{1,25},{9,1},{17,9},{25,17},{2,26},{10... | collective-permute-start | bytes 1032200 | tf_op jit(solution)/shard_map/ppermute | solution.py:34
  4.8 16.7 %collective-permute-start.7 = (bf16[192,896]{1,0:T(8,128)(2,1)}, bf16[192,896]{1,0:T(8,128)(2,1)S(1)}, u32[]{:S(2)}, u32[]{:S(2)}) collective-permute-start(bf16[192,896]{1,0:T(8,128)(2,1)} %get-tuple-element.30.refs_0_), channel_id=1, source_target_pairs={{0,16},{8,24},{16,0},{24,8},{1,17},{9,25},{17,1},{25,9},{2,18},{10... | collective-permute-start | bytes 1032200 | tf_op jit(solution)/shard_map/ppermute | solution.py:34
  5.6 21.8 %collective-permute-start.8 = (bf16[192,896]{1,0:T(8,128)(2,1)}, bf16[192,896]{1,0:T(8,128)(2,1)}, u32[]{:S(2)}, u32[]{:S(2)}) collective-permute-start(bf16[192,896]{1,0:T(8,128)(2,1)} %get-tuple-element.30.refs_0_), channel_id=1, source_target_pairs={{0,8},{8,16},{16,24},{24,0},{1,9},{9,17},{17,25},{25,1},{2,10},{10... | collective-permute-start | bytes 1032200 | tf_op jit(solution)/shard_map/ppermute | solution.py:34
  6.5 20.9 %collective-permute-start.9 = (bf16[192,896]{1,0:T(8,128)(2,1)}, bf16[192,896]{1,0:T(8,128)(2,1)}, u32[]{:S(2)}, u32[]{:S(2)}) collective-permute-start(bf16[192,896]{1,0:T(8,128)(2,1)} %get-tuple-element.31.refs_4_), channel_id=1, source_target_pairs={{0,6},{2,0},{4,2},{6,4},{1,7},{3,1},{5,3},{7,5},{8,14},{10,8},{12,... | collective-permute-start | bytes 1032200 | tf_op jit(solution)/shard_map/ppermute | solution.py:34
  9.5 20.0 %collective-permute-start.10 = (bf16[192,896]{1,0:T(8,128)(2,1)}, bf16[192,896]{1,0:T(8,128)(2,1)}, u32[]{:S(2)}, u32[]{:S(2)}) collective-permute-start(bf16[192,896]{1,0:T(8,128)(2,1)} %get-tuple-element.31.refs_4_), channel_id=1, source_target_pairs={{0,4},{2,6},{4,0},{6,2},{1,5},{3,7},{5,1},{7,3},{8,12},{10,14},{12... | collective-permute-start | bytes 1032200 | tf_op jit(solution)/shard_map/ppermute | solution.py:34
  19.8 9.7 %copy-start.6 = (bf16[192,896]{1,0:T(8,128)(2,1)}, bf16[192,896]{1,0:T(8,128)(2,1)S(1)}, u32[]{:S(2)}) copy-start(bf16[192,896]{1,0:T(8,128)(2,1)S(1)} %collective-permute-done.6.refs_1_) | copy-start | bytes 1032196
  19.8 9.7 %collective-permute-start.11 = (bf16[192,896]{1,0:T(8,128)(2,1)}, bf16[192,896]{1,0:T(8,128)(2,1)}, u32[]{:S(2)}, u32[]{:S(2)}) collective-permute-start(bf16[192,896]{1,0:T(8,128)(2,1)} %get-tuple-element.31.refs_4_), channel_id=1, source_target_pairs={{0,2},{2,4},{4,6},{6,0},{1,3},{3,5},{5,7},{7,1},{8,10},{10,12},{12... | collective-permute-start | bytes 1032200 | tf_op jit(solution)/shard_map/ppermute | solution.py:34
  21.4 45.1 %copy-start.5 = (bf16[128,1024]{1,0:T(8,128)(2,1)}, bf16[128,1024]{1,0:T(8,128)(2,1)S(1)}, u32[]{:S(2)}) copy-start(bf16[128,1024]{1,0:T(8,128)(2,1)S(1)} %pad_maximum_fusion.refs_0_) | copy-start | bytes 786436
  21.5 6.0 %copy-start.7 = (bf16[192,896]{1,0:T(8,128)(2,1)}, bf16[192,896]{1,0:T(8,128)(2,1)S(1)}, u32[]{:S(2)}) copy-start(bf16[192,896]{1,0:T(8,128)(2,1)S(1)} %collective-permute-done.7.refs_2_) | copy-start | bytes 1032196
  21.5 22.6 %collective-permute-start.24 = (bf16[128,1024]{1,0:T(8,128)(2,1)S(1)}, bf16[128,1024]{1,0:T(8,128)(2,1)}, u32[]{:S(2)}, u32[]{:S(2)}) collective-permute-start(bf16[128,1024]{1,0:T(8,128)(2,1)S(1)} %pad_maximum_fusion.refs_0_), channel_id=1, source_target_pairs={{0,193},{64,0},{128,64},{192,128},{1,192},{65,1},{129,65},{193,129... | collective-permute-start | bytes 786440 | tf_op jit(solution)/shard_map/ppermute | solution.py:26
  27.4 18.2 %collective-permute-start.25 = (bf16[128,1024]{1,0:T(8,128)(2,1)S(1)}, bf16[128,1024]{1,0:T(8,128)(2,1)}, u32[]{:S(2)}, u32[]{:S(2)}) collective-permute-start(bf16[128,1024]{1,0:T(8,128)(2,1)S(1)} %pad_maximum_fusion.refs_0_), channel_id=1, source_target_pairs={{0,128},{64,192},{128,1},{192,65},{1,129},{65,193},{129,0},{193,64... | collective-permute-start | bytes 786440 | tf_op jit(solution)/shard_map/ppermute | solution.py:26
  27.4 36.5 %collective-permute-start = (bf16[64,4096]{1,0:T(8,128)(2,1)}, bf16[64,4096]{1,0:T(8,128)(2,1)S(1)}, u32[]{:S(2)}, u32[]{:S(2)}) collective-permute-start(bf16[64,4096]{1,0:T(8,128)(2,1)} %get-tuple-element.24), channel_id=1, source_target_pairs={{0,193},{64,129},{128,65},{192,1},{1,192},{65,128},{129,64},{193,0... | collective-permute-start | bytes 1572872 | tf_op jit(solution)/shard_map/ppermute | solution.py:30
  33.0 41.0 %collective-permute-start.12 = (bf16[2,192,896]{2,1,0:T(8,128)(2,1)}, bf16[2,192,896]{2,1,0:T(8,128)(2,1)}, u32[]{:S(2)}, u32[]{:S(2)}) collective-permute-start(bf16[2,192,896]{2,1,0:T(8,128)(2,1)} %get-tuple-element.32.refs_0_), channel_id=1, source_target_pairs={{0,6},{2,0},{4,2},{6,4},{1,7},{3,1},{5,3},{7,5},{8,14},{10,8},{12,... | collective-permute-start | bytes 2064392 | tf_op jit(solution)/shard_map/ppermute | solution.py:34
  36.7 37.2 %collective-permute-start.13 = (bf16[2,192,896]{2,1,0:T(8,128)(2,1)}, bf16[2,192,896]{2,1,0:T(8,128)(2,1)}, u32[]{:S(2)}, u32[]{:S(2)}) collective-permute-start(bf16[2,192,896]{2,1,0:T(8,128)(2,1)} %get-tuple-element.33.refs_1_), channel_id=1, source_target_pairs={{0,6},{2,0},{4,2},{6,4},{1,7},{3,1},{5,3},{7,5},{8,14},{10,8},{12,... | collective-permute-start | bytes 2064392 | tf_op jit(solution)/shard_map/ppermute | solution.py:34
  44.0 33.2 %collective-permute-start.14 = (bf16[2,192,896]{2,1,0:T(8,128)(2,1)}, bf16[2,192,896]{2,1,0:T(8,128)(2,1)}, u32[]{:S(2)}, u32[]{:S(2)}) collective-permute-start(bf16[2,192,896]{2,1,0:T(8,128)(2,1)} %get-tuple-element.32.refs_0_), channel_id=1, source_target_pairs={{0,2},{2,4},{4,6},{6,0},{1,3},{3,5},{5,7},{7,1},{8,10},{10,12},{12... | collective-permute-start | bytes 2064392 | tf_op jit(solution)/shard_map/ppermute | solution.py:34
  45.6 33.5 %collective-permute-start.15 = (bf16[2,192,896]{2,1,0:T(8,128)(2,1)}, bf16[2,192,896]{2,1,0:T(8,128)(2,1)}, u32[]{:S(2)}, u32[]{:S(2)}) collective-permute-start(bf16[2,192,896]{2,1,0:T(8,128)(2,1)} %get-tuple-element.33.refs_1_), channel_id=1, source_target_pairs={{0,2},{2,4},{4,6},{6,0},{1,3},{3,5},{5,7},{7,1},{8,10},{10,12},{12... | collective-permute-start | bytes 2064392 | tf_op jit(solution)/shard_map/ppermute | solution.py:34
  63.9 0.8 copy-start.3
  64.7 9.2 %collective-permute-start.26 = (bf16[128,1024]{1,0:T(8,128)(2,1)S(1)}, bf16[128,1024]{1,0:T(8,128)(2,1)}, u32[]{:S(2)}, u32[]{:S(2)}) collective-permute-start(bf16[128,1024]{1,0:T(8,128)(2,1)S(1)} %pad_maximum_fusion.refs_0_), channel_id=1, source_target_pairs={{0,64},{64,128},{128,192},{192,1},{1,65},{65,129},{129,193},{193,0... | collective-permute-start | bytes 786440 | tf_op jit(solution)/shard_map/ppermute | solution.py:26
  73.9 31.3 %collective-permute-start.18 = (bf16[2,192,896]{2,1,0:T(8,128)(2,1)}, bf16[2,192,896]{2,1,0:T(8,128)(2,1)}, u32[]{:S(2)}, u32[]{:S(2)}) collective-permute-start(bf16[2,192,896]{2,1,0:T(8,128)(2,1)} %get-tuple-element.34.refs_8_), channel_id=1, source_target_pairs={{0,24},{8,0},{16,8},{24,16},{1,25},{9,1},{17,9},{25,17},{2,26},{10... | collective-permute-start | bytes 2064392 | tf_op jit(solution)/shard_map/ppermute | solution.py:34
  73.9 16.8 %collective-permute-start.1 = (bf16[64,4096]{1,0:T(8,128)(2,1)}, bf16[64,4096]{1,0:T(8,128)(2,1)}, u32[]{:S(2)}, u32[]{:S(2)}) collective-permute-start(bf16[64,4096]{1,0:T(8,128)(2,1)} %get-tuple-element.25), channel_id=1, source_target_pairs={{0,64},{64,128},{128,192},{192,1},{1,65},{65,129},{129,193},{193,0... | collective-permute-start | bytes 1572872 | tf_op jit(solution)/shard_map/ppermute | solution.py:26
  74.0 16.9 %collective-permute-start.2 = (bf16[64,4096]{1,0:T(8,128)(2,1)}, bf16[64,4096]{1,0:T(8,128)(2,1)}, u32[]{:S(2)}, u32[]{:S(2)}) collective-permute-start(bf16[64,4096]{1,0:T(8,128)(2,1)} %get-tuple-element.26), channel_id=1, source_target_pairs={{0,193},{64,0},{128,64},{192,128},{1,192},{65,1},{129,65},{193,129... | collective-permute-start | bytes 1572872 | tf_op jit(solution)/shard_map/ppermute | solution.py:26
  77.2 22.2 %collective-permute-start.3 = (bf16[64,4096]{1,0:T(8,128)(2,1)}, bf16[64,4096]{1,0:T(8,128)(2,1)}, u32[]{:S(2)}, u32[]{:S(2)}) collective-permute-start(bf16[64,4096]{1,0:T(8,128)(2,1)} %get-tuple-element.27), channel_id=1, source_target_pairs={{0,128},{1,129},{192,1},{193,0},{2,130},{3,131},{194,3},{195,2},{4... | collective-permute-start | bytes 1572872 | tf_op jit(solution)/shard_map/ppermute | solution.py:30
  79.1 21.3 %collective-permute-start.4 = (bf16[64,4096]{1,0:T(8,128)(2,1)}, bf16[64,4096]{1,0:T(8,128)(2,1)}, u32[]{:S(2)}, u32[]{:S(2)}) collective-permute-start(bf16[64,4096]{1,0:T(8,128)(2,1)} %get-tuple-element.28), channel_id=1, source_target_pairs={{192,64},{193,65},{0,193},{1,192},{194,66},{195,67},{2,195},{3,194... | collective-permute-start | bytes 1572872 | tf_op jit(solution)/shard_map/ppermute | solution.py:30
  90.8 34.2 %collective-permute-start.27 = (bf16[4,128,1024]{2,1,0:T(8,128)(2,1)}, bf16[4,128,1024]{2,1,0:T(8,128)(2,1)}, u32[]{:S(2)}, u32[]{:S(2)}) collective-permute-start(bf16[4,128,1024]{2,1,0:T(8,128)(2,1)} %stacks.4.mine), channel_id=1, source_target_pairs={{0,32},{32,0},{1,33},{33,1},{2,34},{34,2},{3,35},{35,3},{4,36},{36... | collective-permute-start | bytes 3145736 | tf_op jit(solution)/shard_map/ppermute | solution.py:38
  90.9 24.1 %collective-permute-start.20 = (bf16[2,192,896]{2,1,0:T(8,128)(2,1)}, bf16[2,192,896]{2,1,0:T(8,128)(2,1)}, u32[]{:S(2)}, u32[]{:S(2)}) collective-permute-start(bf16[2,192,896]{2,1,0:T(8,128)(2,1)} %get-tuple-element.34.refs_8_), channel_id=1, source_target_pairs={{0,8},{8,16},{16,24},{24,0},{1,9},{9,17},{17,25},{25,1},{2,10},{10... | collective-permute-start | bytes 2064392 | tf_op jit(solution)/shard_map/ppermute | solution.py:34
  99.4 15.6 %collective-permute-start.19 = (bf16[2,192,896]{2,1,0:T(8,128)(2,1)}, bf16[2,192,896]{2,1,0:T(8,128)(2,1)}, u32[]{:S(2)}, u32[]{:S(2)}) collective-permute-start(bf16[2,192,896]{2,1,0:T(8,128)(2,1)} %get-tuple-element.35.refs_9_), channel_id=1, source_target_pairs={{0,24},{8,0},{16,8},{24,16},{1,25},{9,1},{17,9},{25,17},{2,26},{10... | collective-permute-start | bytes 2064392 | tf_op jit(solution)/shard_map/ppermute | solution.py:34
  100.4 24.6 %collective-permute-start.21 = (bf16[2,192,896]{2,1,0:T(8,128)(2,1)}, bf16[2,192,896]{2,1,0:T(8,128)(2,1)}, u32[]{:S(2)}, u32[]{:S(2)}) collective-permute-start(bf16[2,192,896]{2,1,0:T(8,128)(2,1)} %get-tuple-element.35.refs_9_), channel_id=1, source_target_pairs={{0,8},{8,16},{16,24},{24,0},{1,9},{9,17},{17,25},{25,1},{2,10},{10... | collective-permute-start | bytes 2064392 | tf_op jit(solution)/shard_map/ppermute | solution.py:34
  105.2 72.0 %collective-permute-start.5 = (bf16[256,4096]{1,0:T(8,128)(2,1)}, bf16[256,4096]{1,0:T(8,128)(2,1)}, u32[]{:S(2)}, u32[]{:S(2)}) collective-permute-start(bf16[256,4096]{1,0:T(8,128)(2,1)} %join.1.part), channel_id=1, source_target_pairs={{0,32},{32,0},{1,33},{33,1},{2,34},{34,2},{3,35},{35,3},{4,36},{36... | collective-permute-start | bytes 6291464 | tf_op jit(solution)/shard_map/ppermute | solution.py:38
  115.0 11.5 %collective-permute-start.32 = (bf16[256,1024]{1,0:T(8,128)(2,1)}, bf16[256,1024]{1,0:T(8,128)(2,1)}, u32[]{:S(2)}, u32[]{:S(2)}) collective-permute-start(bf16[256,1024]{1,0:T(8,128)(2,1)} %multiply_convert_fusion.refs_0_), channel_id=1, source_target_pairs={{0,193},{64,0},{128,64},{192,128},{1,192},{65,1},{129,65},{193,129... | collective-permute-start | bytes 1572872 | tf_op jit(solution)/shard_map/ppermute | solution.py:26
  115.0 28.4 %collective-permute-start.33 = (bf16[256,1024]{1,0:T(8,128)(2,1)}, bf16[256,1024]{1,0:T(8,128)(2,1)}, u32[]{:S(2)}, u32[]{:S(2)}) collective-permute-start(bf16[256,1024]{1,0:T(8,128)(2,1)} %multiply_convert_fusion.refs_0_), channel_id=1, source_target_pairs={{0,128},{64,192},{128,1},{192,65},{1,129},{65,193},{129,0},{193,64... | collective-permute-start | bytes 1572872 | tf_op jit(solution)/shard_map/ppermute | solution.py:26
  125.0 25.8 %collective-permute-start.34 = (bf16[256,1024]{1,0:T(8,128)(2,1)}, bf16[256,1024]{1,0:T(8,128)(2,1)}, u32[]{:S(2)}, u32[]{:S(2)}) collective-permute-start(bf16[256,1024]{1,0:T(8,128)(2,1)} %multiply_convert_fusion.refs_0_), channel_id=1, source_target_pairs={{0,64},{64,128},{128,192},{192,1},{1,65},{65,129},{129,193},{193,0... | collective-permute-start | bytes 1572872 | tf_op jit(solution)/shard_map/ppermute | solution.py:26
  125.0 30.4 %collective-permute-start.16 = (bf16[2,192,896]{2,1,0:T(8,128)(2,1)}, bf16[2,192,896]{2,1,0:T(8,128)(2,1)S(1)}, u32[]{:S(2)}, u32[]{:S(2)}) collective-permute-start(bf16[2,192,896]{2,1,0:T(8,128)(2,1)} %collective-permute-done.14.refs_4_), channel_id=1, source_target_pairs={{0,2},{2,4},{4,6},{6,0},{1,3},{3,5},{5,7},{7,1},{8,10},{10,12},{12... | collective-permute-start | bytes 2064392 | tf_op jit(solution)/shard_map/ppermute | solution.py:34
  126.5 29.1 %collective-permute-start.17 = (bf16[2,192,896]{2,1,0:T(8,128)(2,1)}, bf16[2,192,896]{2,1,0:T(8,128)(2,1)S(1)}, u32[]{:S(2)}, u32[]{:S(2)}) collective-permute-start(bf16[2,192,896]{2,1,0:T(8,128)(2,1)} %collective-permute-done.13.refs_3_), channel_id=1, source_target_pairs={{0,6},{2,0},{4,2},{6,4},{1,7},{3,1},{5,3},{7,5},{8,14},{10,8},{12,... | collective-permute-start | bytes 2064392 | tf_op jit(solution)/shard_map/ppermute | solution.py:34
  143.3 12.5 %collective-permute-start.22 = (bf16[2,192,896]{2,1,0:T(8,128)(2,1)}, bf16[2,192,896]{2,1,0:T(8,128)(2,1)}, u32[]{:S(2)}, u32[]{:S(2)}) collective-permute-start(bf16[2,192,896]{2,1,0:T(8,128)(2,1)} %collective-permute-done.20.refs_12_), channel_id=1, source_target_pairs={{0,8},{8,16},{16,24},{24,0},{1,9},{9,17},{17,25},{25,1},{2,10},{10... | collective-permute-start | bytes 2064392 | tf_op jit(solution)/shard_map/ppermute | solution.py:34
  150.8 17.7 %collective-permute-start.23 = (bf16[2,192,896]{2,1,0:T(8,128)(2,1)}, bf16[2,192,896]{2,1,0:T(8,128)(2,1)}, u32[]{:S(2)}, u32[]{:S(2)}) collective-permute-start(bf16[2,192,896]{2,1,0:T(8,128)(2,1)} %collective-permute-done.19.refs_11_), channel_id=1, source_target_pairs={{0,24},{8,0},{16,8},{24,16},{1,25},{9,1},{17,9},{25,17},{2,26},{10... | collective-permute-start | bytes 2064392 | tf_op jit(solution)/shard_map/ppermute | solution.py:34
  155.4 13.0 %copy-start.1 = (bf16[2,192,896]{2,1,0:T(8,128)(2,1)}, bf16[2,192,896]{2,1,0:T(8,128)(2,1)S(1)}, u32[]{:S(2)}) copy-start(bf16[2,192,896]{2,1,0:T(8,128)(2,1)S(1)} %collective-permute-done.16.refs_6_) | copy-start | bytes 2064388
  155.5 69.1 %collective-permute-start.35 = (bf16[4,256,1024]{2,1,0:T(8,128)(2,1)}, bf16[4,256,1024]{2,1,0:T(8,128)(2,1)}, u32[]{:S(2)}, u32[]{:S(2)}) collective-permute-start(bf16[4,256,1024]{2,1,0:T(8,128)(2,1)} %stacks.5.mine), channel_id=1, source_target_pairs={{0,32},{32,0},{1,33},{33,1},{2,34},{34,2},{3,35},{35,3},{4,36},{36... | collective-permute-start | bytes 6291464 | tf_op jit(solution)/shard_map/ppermute | solution.py:38
  155.6 12.9 %copy-start.2 = (bf16[2,192,896]{2,1,0:T(8,128)(2,1)}, bf16[2,192,896]{2,1,0:T(8,128)(2,1)S(1)}, u32[]{:S(2)}) copy-start(bf16[2,192,896]{2,1,0:T(8,128)(2,1)S(1)} %collective-permute-done.17.refs_7_) | copy-start | bytes 2064388
  173.0 19.7 %collective-permute-start.28 = (bf16[512,256]{1,0:T(8,128)(2,1)}, bf16[512,256]{1,0:T(8,128)(2,1)S(1)}, u32[]{:S(2)}, u32[]{:S(2)}) collective-permute-start(bf16[512,256]{1,0:T(8,128)(2,1)} %down_proj.1.w0), channel_id=1, source_target_pairs={{0,6},{2,0},{4,2},{6,4},{1,7},{3,1},{5,3},{7,5},{8,14},{10,8},{12,... | collective-permute-start | bytes 786440 | tf_op jit(solution)/shard_map/ppermute | solution.py:34
  176.1 16.7 %collective-permute-start.29 = (bf16[512,256]{1,0:T(8,128)(2,1)}, bf16[512,256]{1,0:T(8,128)(2,1)S(1)}, u32[]{:S(2)}, u32[]{:S(2)}) collective-permute-start(bf16[512,256]{1,0:T(8,128)(2,1)} %down_proj.1.w0), channel_id=1, source_target_pairs={{0,4},{2,6},{4,0},{6,2},{1,5},{3,7},{5,1},{7,3},{8,12},{10,14},{12... | collective-permute-start | bytes 786440 | tf_op jit(solution)/shard_map/ppermute | solution.py:34
  176.3 16.5 %collective-permute-start.30 = (bf16[512,256]{1,0:T(8,128)(2,1)}, bf16[512,256]{1,0:T(8,128)(2,1)S(1)}, u32[]{:S(2)}, u32[]{:S(2)}) collective-permute-start(bf16[512,256]{1,0:T(8,128)(2,1)} %down_proj.1.w0), channel_id=1, source_target_pairs={{0,2},{2,4},{4,6},{6,0},{1,3},{3,5},{5,7},{7,1},{8,10},{10,12},{12... | collective-permute-start | bytes 786440 | tf_op jit(solution)/shard_map/ppermute | solution.py:34
  192.8 0.7 copy-start.8
  192.8 0.8 copy-start.9
  193.6 0.7 copy-start.10
  197.3 26.4 %copy-start.11 = (s32[256]{0:T(256)S(1)}, s32[256]{0:T(256)}, u32[]{:S(2)}) copy-start(s32[256]{0:T(256)} %param.17) | copy-start | bytes 3076
  197.3 2.1 collective-permute-start.31
  217.6 16.2 %all-to-all-start.1 = ((bf16[16,16,1024]{2,1,0:T(8,128)(2,1)}), bf16[16,16,1024]{2,1,0:T(8,128)(2,1)S(1)}, u32[]{:S(2)}, u32[]{:S(2)}) async-start(bf16[16,16,1024]{2,1,0:T(8,128)(2,1)} %candidates.1), calls=%async_computation.1 | async-start | bytes 1048576 | tf_op jit(solution)/shard_map/all_to_all | solution.py:497
  233.8 0.8 copy-start.4
where the time goes:
time: 284 us; the launch traced here: 281 us
  waiting for transfers between devices  108 us (38%)
  starting transfers between devices  56.7 us (20%)
  Pallas kernels  53.1 us (19%)
  blocking collectives  50.9 us (18%)
  local copies, waits for them, and re-layouts  4.88 us (2%)
  matrix products  4.51 us (2%)
    ppermute x21, waiting for transfers between devices, shift(): return lax.ppermute(a, axis, [(i, (i + k) % 4) for i in range(4)])  41.1 us
    ppermute x8, waiting for transfers between devices, shift_z(): lax.ppermute(a, ('zl', 'zh'), z_pairs([(z, z + k) for z in range(8)]))  31.8 us
    ppermute x21, starting transfers between devices, shift(): return lax.ppermute(a, axis, [(i, (i + k) % 4) for i in range(4)])  30.1 us
    ppermute x3, waiting for transfers between devices, send_z(): return lax.ppermute(a, ('zl', 'zh'), z_pairs(pairs))  23.9 us
    all_to_all x1, blocking collectives, shards(): notes = lax.all_to_all(note, ('zl', 'core', 'zh'), 0, 0)  18.6 us
    all_to_all x1, blocking collectives, shards(): lax.all_to_all(vote(notes, kernel), ('zl', 'core', 'x', 'y'), 0, 0)  17.1 us
    pallas_call x1, Pallas kernels, feed_forward(): pl.pallas_call(ff_kernel, out_shape=jax.ShapeDtypeStruct((256, 512), BF16...  15.5 us
    all_to_all x1, blocking collectives, shards(): emb = lax.all_to_all(emb, ('zl', 'zh'), 0, 0)  15.2 us
  transfers between devices with their start and end apart: 37, of which 13 were waited for; matrix products, arithmetic and copies ran while one was open for 3% of the time, Pallas kernels for 14%

commit v1 on v0

--- a/solution.py
+++ b/solution.py
@@ -335,6 +335,25 @@
     return (matrix * lax.rsqrt(jnp.sum(matrix * matrix, axis=1, keepdims=True) + 1e-06)).astype(BF16)
 
 
+def encode_kernel(rows, enc, out):
+    out[...] = unit_rows(jnp.dot(rows[...], enc[...], preferred_element_type=F32))
+
+
+def encode(rows, enc):
+    n, d = rows.shape
+    return pl.pallas_call(
+        encode_kernel,
+        out_shape=jax.ShapeDtypeStruct((n, enc.shape[1]), BF16),
+        grid=(2,),
+        in_specs=[
+            pl.BlockSpec((n // 2, d), lambda i: (i, 0)),
+            pl.BlockSpec(enc.shape, lambda i: (0, 0)),
+        ],
+        out_specs=pl.BlockSpec((n // 2, enc.shape[1]), lambda i: (i, 0)),
+        name="encode",
+    )(rows, enc)
+
+
 def candidate_kernel(parts, out):
     total = parts[0].astype(F32)
     for i in range(1, 8):
@@ -471,7 +490,7 @@
     state_cols = lax.dynamic_slice_in_dim(states, (zl * 2 + core) * 512, 512, 1)
     resid = jnp.dot(pool, state_cols, preferred_element_type=F32).astype(BF16)
     resid = jnp.dot(resid, proj, preferred_element_type=F32)
-    encoded = unit_rows(jnp.dot(rows, enc, preferred_element_type=F32))
+    encoded = encode(rows, enc)
     (cols,) = stacks((cols, *near_cols))
     cols_other = swap_core(cols)
     far = []

time: 284 us -> 286 us (level)
  starting transfers between devices: 56.7 us -> 53.2 us
  Pallas kernels: 53.1 us -> 56.5 us
  waiting for transfers between devices: 108 us -> 111 us
    ppermute x8, waiting for transfers between devices: 31.8 us -> 39.6 us  [shift_z(): lax.ppermute(a, ('zl', 'zh'), z_pairs([(z, z + k) for z in range(8)]))]
    ppermute x21, waiting for transfers between devices: 41.1 us -> 35.1 us  [shift(): return lax.ppermute(a, axis, [(i, (i + k) % 4) for i in range(4)])]
    pallas_call x0 -> x1, Pallas kernels: none -> 3.51 us  [encode(): pl.pallas_call(encode_kernel, out_shape=jax.ShapeDtypeStruct((n, enc.shap...]
  transfers between devices with their start and end apart: 37 -> 37, of which waited for: 13 -> 14; matrix products, arithmetic and copies ran while one was open for 3% -> 2% of each run, Pallas kernels for 14% -> 15%
where the time goes in v1:
time: 286 us; the launch traced here: 282 us
  waiting for transfers between devices  111 us (39%)
  Pallas kernels  56.5 us (20%)
  starting transfers between devices  53.2 us (19%)
  blocking collectives  50.8 us (18%)
  local copies, waits for them, and re-layouts  6.27 us (2%)
    ppermute x8, waiting for transfers between devices, shift_z(): lax.ppermute(a, ('zl', 'zh'), z_pairs([(z, z + k) for z in range(8)]))  39.6 us
    ppermute x21, waiting for transfers between devices, shift(): return lax.ppermute(a, axis, [(i, (i + k) % 4) for i in range(4)])  35.1 us
    ppermute x21, starting transfers between devices, shift(): return lax.ppermute(a, axis, [(i, (i + k) % 4) for i in range(4)])  27.5 us
    ppermute x3, waiting for transfers between devices, send_z(): return lax.ppermute(a, ('zl', 'zh'), z_pairs(pairs))  24.4 us
    all_to_all x1, blocking collectives, shards(): notes = lax.all_to_all(note, ('zl', 'core', 'zh'), 0, 0)  18.6 us
    all_to_all x1, blocking collectives, shards(): lax.all_to_all(vote(notes, kernel), ('zl', 'core', 'x', 'y'), 0, 0)  17.1 us
    pallas_call x1, Pallas kernels, feed_forward(): pl.pallas_call(ff_kernel, out_shape=jax.ShapeDtypeStruct((256, 512), BF16...  15.5 us
    all_to_all x1, blocking collectives, shards(): emb = lax.all_to_all(emb, ('zl', 'zh'), 0, 0)  15.1 us
  transfers between devices with their start and end apart: 37, of which 14 were waited for; matrix products, arithmetic and copies ran while one was open for 2% of the time, Pallas kernels for 15%

profile of v1, /device:TPU:0, one launch (start us, length us, event | category | flops | bytes accessed | tf_op | source)
XLA Modules:
  0.0 282.2 jit_solution(5878597036486811623)
XLA Ops:
  0.0 3.5 %pack_weights.1 = (bf16[192,896]{1,0:T(8,128)(2,1)}, bf16[192,896]{1,0:T(8,128)(2,1)}, bf16[64,4096]{1,0:T(8,128)(2,1)}) custom-call(bf16[256,896]{1,0:T(8,128)(2,1)} %gate.1, bf16[256,896]{1,0:T(8,128)(2,1)} %up.1, bf16[896,256]{1,0:T(8,128)(2,1)} %down.1, f32[32,128]{1,0:T(8,128)} %bitcast.11, bf16[512,4096]{1,0:T(8,128)(2,1)} %own.1), custom_call_target="tpu_custom_call" | custom-call | tf_op jit(solution)/shard_map/pack_weights/pallas_call | solution.py:69
  3.5 1.1 collective-permute-start.6
  4.6 0.8 collective-permute-start.7
  5.4 0.9 collective-permute-start.8
  6.3 3.0 %collective-permute-start.9 = (bf16[192,896]{1,0:T(8,128)(2,1)}, bf16[192,896]{1,0:T(8,128)(2,1)S(1)}, u32[]{:S(2)}, u32[]{:S(2)}) collective-permute-start(bf16[192,896]{1,0:T(8,128)(2,1)} %get-tuple-element.31.refs_4_), channel_id=1, source_target_pairs={{0,6},{2,0},{4,2},{6,4},{1,7},{3,1},{5,3},{7,5},{8,14},{10,8},{12,... | collective-permute-start | bytes 1032200 | tf_op jit(solution)/shard_map/ppermute | solution.py:34
  9.3 0.6 collective-permute-start.10
  9.9 1.0 constant_dynamic-slice_fusion
  10.9 8.7 %collective-permute-done.6.refs_1_ = bf16[192,896]{1,0:T(8,128)(2,1)S(1)} collective-permute-done((bf16[192,896]{1,0:T(8,128)(2,1)}, bf16[192,896]{1,0:T(8,128)(2,1)S(1)}, u32[]{:S(2)}, u32[]{:S(2)}) %collective-permute-start.6) | collective-permute-done | bytes 344096 | tf_op jit(solution)/shard_map/ppermute | solution.py:34
  19.6 1.6 collective-permute-start.11
  21.2 0.7 pad_maximum_fusion.refs_0_
  22.0 5.9 %collective-permute-start.24 = (bf16[128,1024]{1,0:T(8,128)(2,1)}, bf16[128,1024]{1,0:T(8,128)(2,1)S(1)}, u32[]{:S(2)}, u32[]{:S(2)}) collective-permute-start(bf16[128,1024]{1,0:T(8,128)(2,1)} %pad_maximum_fusion.refs_0_), channel_id=1, source_target_pairs={{0,193},{64,0},{128,64},{192,128},{1,192},{65,1},{129,65},{193,129... | collective-permute-start | bytes 786440 | tf_op jit(solution)/shard_map/ppermute | solution.py:26
  27.9 1.5 collective-permute-start
  29.4 0.7 copy-done.14
  30.1 0.7 copy-done.15
  30.8 3.4 %stacks.3 = (bf16[2,192,896]{2,1,0:T(8,128)(2,1)}, bf16[2,192,896]{2,1,0:T(8,128)(2,1)}, bf16[2,192,896]{2,1,0:T(8,128)(2,1)}, bf16[2,192,896]{2,1,0:T(8,128)(2,1)}) custom-call(bf16[192,896]{1,0:T(8,128)(2,1)} %get-tuple-element.30.refs_0_, bf16[192,896]{1,0:T(8,128)(2,1)} %copy-done.10, bf16[192,896]{1,0:T(8,128)(2,1)} %copy-done.11, ...), custom_call_target="tpu_custom_call" | custom-call | tf_op jit(solution)/shard_map/stacks/pallas_call | solution.py:100
  34.2 3.7 %collective-permute-start.12 = (bf16[2,192,896]{2,1,0:T(8,128)(2,1)}, bf16[2,192,896]{2,1,0:T(8,128)(2,1)S(1)}, u32[]{:S(2)}, u32[]{:S(2)}) collective-permute-start(bf16[2,192,896]{2,1,0:T(8,128)(2,1)} %get-tuple-element.32.refs_0_), channel_id=1, source_target_pairs={{0,6},{2,0},{4,2},{6,4},{1,7},{3,1},{5,3},{7,5},{8,14},{10,8},{12,... | collective-permute-start | bytes 2064392 | tf_op jit(solution)/shard_map/ppermute | solution.py:34
  38.0 7.7 %collective-permute-done.24.refs_1_ = bf16[128,1024]{1,0:T(8,128)(2,1)S(1)} collective-permute-done((bf16[128,1024]{1,0:T(8,128)(2,1)}, bf16[128,1024]{1,0:T(8,128)(2,1)S(1)}, u32[]{:S(2)}, u32[]{:S(2)}) %collective-permute-start.24) | collective-permute-done | bytes 262176 | tf_op jit(solution)/shard_map/ppermute | solution.py:26
  45.7 1.6 collective-permute-start.14
  47.3 1.0 collective-permute-start.15
  48.3 15.6 %collective-permute-done.q = bf16[64,4096]{1,0:T(8,128)(2,1)S(1)} collective-permute-done((bf16[64,4096]{1,0:T(8,128)(2,1)}, bf16[64,4096]{1,0:T(8,128)(2,1)S(1)}, u32[]{:S(2)}, u32[]{:S(2)}) %collective-permute-start) | collective-permute-done | bytes 524320 | tf_op jit(solution)/shard_map/ppermute | solution.py:30
  63.9 0.8 copy-done.8
  64.7 2.9 %relay.1 = (bf16[64,4096]{1,0:T(8,128)(2,1)}, bf16[64,4096]{1,0:T(8,128)(2,1)}, bf16[64,4096]{1,0:T(8,128)(2,1)}, bf16[64,4096]{1,0:T(8,128)(2,1)}) custom-call(bf16[512,4096]{1,0:T(8,128)(2,1)} %own.1, bf16[64,4096]{1,0:T(8,128)(2,1)} %copy-done.8), custom_call_target="tpu_custom_call" | custom-call | tf_op jit(solution)/shard_map/relay/pallas_call | solution.py:142
  67.6 5.7 %collective-permute-done.26.refs_3_ = bf16[128,1024]{1,0:T(8,128)(2,1)} collective-permute-done((bf16[128,1024]{1,0:T(8,128)(2,1)}, bf16[128,1024]{1,0:T(8,128)(2,1)}, u32[]{:S(2)}, u32[]{:S(2)}) %collective-permute-start.26) | collective-permute-done | bytes 262176 | tf_op jit(solution)/shard_map/ppermute | solution.py:26
  73.3 3.2 %collective-permute-start.2 = (bf16[64,4096]{1,0:T(8,128)(2,1)}, bf16[64,4096]{1,0:T(8,128)(2,1)}, u32[]{:S(2)}, u32[]{:S(2)}) collective-permute-start(bf16[64,4096]{1,0:T(8,128)(2,1)} %get-tuple-element.26), channel_id=1, source_target_pairs={{0,193},{64,0},{128,64},{192,128},{1,192},{65,1},{129,65},{193,129... | collective-permute-start | bytes 1572872 | tf_op jit(solution)/shard_map/ppermute | solution.py:26
  76.5 1.9 collective-permute-start.3
  78.5 7.0 %collective-permute-start.4 = (bf16[64,4096]{1,0:T(8,128)(2,1)}, bf16[64,4096]{1,0:T(8,128)(2,1)}, u32[]{:S(2)}, u32[]{:S(2)}) collective-permute-start(bf16[64,4096]{1,0:T(8,128)(2,1)} %get-tuple-element.28), channel_id=1, source_target_pairs={{192,64},{193,65},{0,193},{1,192},{194,66},{195,67},{2,195},{3,194... | collective-permute-start | bytes 1572872 | tf_op jit(solution)/shard_map/ppermute | solution.py:30
  85.7 2.2 stacks.4.mine
  87.9 1.7 collective-permute-done.1.p1
  89.9 8.8 %collective-permute-done.3.p3 = bf16[64,4096]{1,0:T(8,128)(2,1)} collective-permute-done((bf16[64,4096]{1,0:T(8,128)(2,1)}, bf16[64,4096]{1,0:T(8,128)(2,1)}, u32[]{:S(2)}, u32[]{:S(2)}) %collective-permute-start.3) | collective-permute-done | bytes 524320 | tf_op jit(solution)/shard_map/ppermute | solution.py:30
  98.7 2.0 collective-permute-start.21
  100.7 2.7 fusion.resid
  103.4 3.5 %encode.1.refs_0_ = bf16[256,1024]{1,0:T(8,128)(2,1)} custom-call(bf16[256,1024]{1,0:T(8,128)(2,1)} %rows.1, bf16[1024,1024]{1,0:T(8,128)(2,1)} %enc.1), custom_call_target="tpu_custom_call" | custom-call | tf_op jit(solution)/shard_map/encode/pallas_call | solution.py:344
  106.9 2.9 %join.1.part = bf16[256,4096]{1,0:T(8,128)(2,1)} custom-call(bf16[64,4096]{1,0:T(8,128)(2,1)} %copy-done.8, bf16[64,4096]{1,0:T(8,128)(2,1)} %collective-permute-done.1.p1, bf16[64,4096]{1,0:T(8,128)(2,1)} %collective-permute-done.2.p2, bf16[64,4096]{1,0:T(8,128)(2,1)} %collective-permute-done.3.p3, bf16[64,4096]{1,0:T(8,128)(2,1)} %collective-permute-done.4.p4), custom_call_target="tpu_custom_call" | custom-call | tf_op jit(solution)/shard_map/join/pallas_call | solution.py:154
  110.0 5.4 %collective-permute-done.19.refs_11_ = bf16[2,192,896]{2,1,0:T(8,128)(2,1)} collective-permute-done((bf16[2,192,896]{2,1,0:T(8,128)(2,1)S(1)}, bf16[2,192,896]{2,1,0:T(8,128)(2,1)}, u32[]{:S(2)}, u32[]{:S(2)}) %collective-permute-start.19) | collective-permute-done | bytes 688160 | tf_op jit(solution)/shard_map/ppermute | solution.py:34
  115.3 8.2 %collective-permute-done.21.refs_13_ = bf16[2,192,896]{2,1,0:T(8,128)(2,1)} collective-permute-done((bf16[2,192,896]{2,1,0:T(8,128)(2,1)S(1)}, bf16[2,192,896]{2,1,0:T(8,128)(2,1)}, u32[]{:S(2)}, u32[]{:S(2)}) %collective-permute-start.21) | collective-permute-done | bytes 688160 | tf_op jit(solution)/shard_map/ppermute | solution.py:34
  123.5 1.5 collective-permute-start.16
  125.1 2.7 collective-permute-done.32.refs_1_
  127.8 2.8 collective-permute-start.17
  130.6 13.1 %collective-permute-done.33.refs_2_ = bf16[256,1024]{1,0:T(8,128)(2,1)} collective-permute-done((bf16[256,1024]{1,0:T(8,128)(2,1)}, bf16[256,1024]{1,0:T(8,128)(2,1)}, u32[]{:S(2)}, u32[]{:S(2)}) %collective-permute-start.33) | collective-permute-done | bytes 524320 | tf_op jit(solution)/shard_map/ppermute | solution.py:26
  143.7 8.7 %collective-permute-done.34.refs_3_ = bf16[256,1024]{1,0:T(8,128)(2,1)} collective-permute-done((bf16[256,1024]{1,0:T(8,128)(2,1)}, bf16[256,1024]{1,0:T(8,128)(2,1)}, u32[]{:S(2)}, u32[]{:S(2)}) %collective-permute-start.34) | collective-permute-done | bytes 524320 | tf_op jit(solution)/shard_map/ppermute | solution.py:26
  152.4 1.8 collective-permute-start.23
  154.1 2.9 %stacks.5.mine = bf16[4,256,1024]{2,1,0:T(8,128)(2,1)} custom-call(bf16[256,1024]{1,0:T(8,128)(2,1)} %encode.1.refs_0_, bf16[256,1024]{1,0:T(8,128)(2,1)} %collective-permute-done.32.refs_1_, bf16[256,1024]{1,0:T(8,128)(2,1)} %collective-permute-done.33.refs_2_, bf16[256,1024]{1,0:T(8,128)(2,1)} %collective-permute-done.34.refs_3_), custom_call_target="tpu_custom_call" | custom-call | tf_op jit(solution)/shard_map/stacks/pallas_call | solution.py:100
  157.2 12.8 %collective-permute-done.23.refs_15_ = bf16[2,192,896]{2,1,0:T(8,128)(2,1)} collective-permute-done((bf16[2,192,896]{2,1,0:T(8,128)(2,1)}, bf16[2,192,896]{2,1,0:T(8,128)(2,1)}, u32[]{:S(2)}, u32[]{:S(2)}) %collective-permute-start.23) | collective-permute-done | bytes 688160 | tf_op jit(solution)/shard_map/ppermute | solution.py:34
  170.1 4.6 %down_proj.1.w0 = bf16[512,256]{1,0:T(8,128)(2,1)} custom-call(bf16[4,128,1024]{2,1,0:T(8,128)(2,1)} %stacks.4.mine, bf16[4,128,1024]{2,1,0:T(8,128)(2,1)} %collective-permute-done.27.theirs, bf16[2,192,896]{2,1,0:T(8,128)(2,1)} %get-tuple-element.32.refs_0_, bf16[2,192,896]{2,1,0:T(8,128)(2,1)} %get-tuple-element.33.refs_1_, ...), custom_call_target="tpu_custom_call" | custom-call | tf_op jit(solution)/shard_map/down_proj/pallas_call | solution.py:297
  174.6 2.8 collective-permute-start.28
  177.5 0.6 collective-permute-start.29
  178.1 1.0 collective-permute-start.30
  179.0 15.5 %feed_forward.1.hp = bf16[256,512]{1,0:T(8,128)(2,1)} custom-call(bf16[512,4096]{1,0:T(8,128)(2,1)} %own.1, bf16[256,4096]{1,0:T(8,128)(2,1)} %join.1.part, bf16[256,4096]{1,0:T(8,128)(2,1)} %collective-permute-done.5.other, bf16[2,192,896]{2,1,0:T(8,128)(2,1)} %get-tuple-element.32.refs_0_, bf16[2,192,896]{2,1,0:T(8,128)(2,1)} %get-tuple-element.33.refs_1_, ...), custom_call_target="tpu_custom_call" | custom-call | tf_op jit(solution)/shard_map/feed_forward/pallas_call | solution.py:261
  194.6 0.7 copy-done.16
  195.4 0.7 copy-done.18
  196.1 3.1 %embed.1 = (f32[128,1024]{1,0:T(8,128)}, f32[128,1024]{1,0:T(8,128)}) custom-call(bf16[256,512]{1,0:T(8,128)(2,1)} %feed_forward.1.hp, bf16[512,256]{1,0:T(8,128)(2,1)} %down_proj.1.w0, bf16[512,256]{1,0:T(8,128)(2,1)} %copy-done.16, bf16[512,256]{1,0:T(8,128)(2,1)} %copy-done.17, bf16[512,256]{1,0:T(8,128)(2,1)} %copy-done.18, f32[128,1024]{1,0:T(8,128)} %fusion.resid), custom_call_target="tpu_custom_call" | custom-call | tf_op jit(solution)/shard_map/embed/pallas_call | solution.py:324
  199.2 2.1 collective-permute-done.31
  201.3 1.1 add_convert_fusion
  202.4 15.1 %all_to_all.20.parts = bf16[8,16,1024]{2,1,0:T(8,128)(2,1)} all-to-all(bf16[8,16,1024]{2,1,0:T(8,128)(2,1)S(1)} %bitcast.10), channel_id=1, replica_groups=mesh['zl'=4,'core'=2,'x'=4,'y'=4,'zh'=2] {'zl','zh'}, dimensions={0} | all-to-all | bytes 524288 | tf_op jit(solution)/shard_map/all_to_all | solution.py:512
  217.5 1.9 candidates.1
  219.4 6.0 %all-to-all-start.1 = ((bf16[16,16,1024]{2,1,0:T(8,128)(2,1)}), bf16[16,16,1024]{2,1,0:T(8,128)(2,1)S(1)}, u32[]{:S(2)}, u32[]{:S(2)}) async-start(bf16[16,16,1024]{2,1,0:T(8,128)(2,1)} %candidates.1), calls=%async_computation.1 | async-start | bytes 1048576 | tf_op jit(solution)/shard_map/all_to_all | solution.py:516
  225.4 0.8 copy.11.ids_col
  226.2 9.3 %all-to-all-done.1 = bf16[16,16,1024]{2,1,0:T(8,128)(2,1)S(1)} async-done(((bf16[16,16,1024]{2,1,0:T(8,128)(2,1)}), bf16[16,16,1024]{2,1,0:T(8,128)(2,1)S(1)}, u32[]{:S(2)}, u32[]{:S(2)}) %all-to-all-start.1) | async-done | bytes 524320 | tf_op jit(solution)/shard_map/all_to_all | solution.py:516
  235.5 0.8 copy-done.9
  236.3 5.9 %score.1 = (f32[256,2048]{1,0:T(8,128)}, f32[16,16,256]{2,1,0:T(8,128)}) custom-call(bf16[256,1024]{1,0:T(8,128)(2,1)} %bitcast.9, bf16[4,256,1024]{2,1,0:T(8,128)(2,1)} %stacks.5.mine, bf16[4,256,1024]{2,1,0:T(8,128)(2,1)} %collective-permute-done.35.theirs, s32[1,256]{1,0:T(1,128)} %bitcast.12, s32[256,1]{1,0:T(8,128)} %copy.11.ids_col), custom_call_target="tpu_custom_call" | custom-call | tf_op jit(solution)/shard_map/score/pallas_call | solution.py:403
  242.2 18.6 %all_to_all.21.notes = f32[16,16,256]{2,1,0:T(8,128)} all-to-all(f32[16,16,256]{2,1,0:T(8,128)} %get-tuple-element.41), channel_id=1, replica_groups=mesh['zl'=4,'core'=2,'x'=4,'y'=4,'zh'=2] {'zl','core','zh'}, dimensions={0} | all-to-all | bytes 524288 | tf_op jit(solution)/shard_map/all_to_all | solution.py:518
  260.8 2.6 vote.1
  263.4 17.1 %all_to_all.22.parts = f32[128,2,128]{2,1,0:T(2,128)} all-to-all(f32[128,2,128]{2,1,0:T(2,128)} %vote.1), channel_id=1, replica_groups=mesh['zl'=4,'core'=2,'x'=4,'y'=4,'zh'=2] {'zl','core','x','y'}, dimensions={0} | all-to-all | bytes 262144 | tf_op jit(solution)/shard_map/all_to_all | solution.py:519
  280.5 1.7 gather_votes.1
  (75 shorter events, 1.1 us)
Async XLA Ops:
  3.5 16.1 %collective-permute-start.6 = (bf16[192,896]{1,0:T(8,128)(2,1)}, bf16[192,896]{1,0:T(8,128)(2,1)S(1)}, u32[]{:S(2)}, u32[]{:S(2)}) collective-permute-start(bf16[192,896]{1,0:T(8,128)(2,1)} %get-tuple-element.30.refs_0_), channel_id=1, source_target_pairs={{0,24},{8,0},{16,8},{24,16},{1,25},{9,1},{17,9},{25,17},{2,26},{10... | collective-permute-start | bytes 1032200 | tf_op jit(solution)/shard_map/ppermute | solution.py:34
  4.6 17.4 %collective-permute-start.7 = (bf16[192,896]{1,0:T(8,128)(2,1)}, bf16[192,896]{1,0:T(8,128)(2,1)S(1)}, u32[]{:S(2)}, u32[]{:S(2)}) collective-permute-start(bf16[192,896]{1,0:T(8,128)(2,1)} %get-tuple-element.30.refs_0_), channel_id=1, source_target_pairs={{0,16},{8,24},{16,0},{24,8},{1,17},{9,25},{17,1},{25,9},{2,18},{10... | collective-permute-start | bytes 1032200 | tf_op jit(solution)/shard_map/ppermute | solution.py:34
  5.4 22.4 %collective-permute-start.8 = (bf16[192,896]{1,0:T(8,128)(2,1)}, bf16[192,896]{1,0:T(8,128)(2,1)S(1)}, u32[]{:S(2)}, u32[]{:S(2)}) collective-permute-start(bf16[192,896]{1,0:T(8,128)(2,1)} %get-tuple-element.30.refs_0_), channel_id=1, source_target_pairs={{0,8},{8,16},{16,24},{24,0},{1,9},{9,17},{17,25},{25,1},{2,10},{10... | collective-permute-start | bytes 1032200 | tf_op jit(solution)/shard_map/ppermute | solution.py:34
  6.3 21.6 %collective-permute-start.9 = (bf16[192,896]{1,0:T(8,128)(2,1)}, bf16[192,896]{1,0:T(8,128)(2,1)S(1)}, u32[]{:S(2)}, u32[]{:S(2)}) collective-permute-start(bf16[192,896]{1,0:T(8,128)(2,1)} %get-tuple-element.31.refs_4_), channel_id=1, source_target_pairs={{0,6},{2,0},{4,2},{6,4},{1,7},{3,1},{5,3},{7,5},{8,14},{10,8},{12,... | collective-permute-start | bytes 1032200 | tf_op jit(solution)/shard_map/ppermute | solution.py:34
  9.3 20.0 %collective-permute-start.10 = (bf16[192,896]{1,0:T(8,128)(2,1)}, bf16[192,896]{1,0:T(8,128)(2,1)S(1)}, u32[]{:S(2)}, u32[]{:S(2)}) collective-permute-start(bf16[192,896]{1,0:T(8,128)(2,1)} %get-tuple-element.31.refs_4_), channel_id=1, source_target_pairs={{0,4},{2,6},{4,0},{6,2},{1,5},{3,7},{5,1},{7,3},{8,12},{10,14},{12... | collective-permute-start | bytes 1032200 | tf_op jit(solution)/shard_map/ppermute | solution.py:34
  19.6 9.7 %copy-start.10 = (bf16[192,896]{1,0:T(8,128)(2,1)}, bf16[192,896]{1,0:T(8,128)(2,1)S(1)}, u32[]{:S(2)}) copy-start(bf16[192,896]{1,0:T(8,128)(2,1)S(1)} %collective-permute-done.6.refs_1_) | copy-start | bytes 1032196
  19.6 9.7 %collective-permute-start.11 = (bf16[192,896]{1,0:T(8,128)(2,1)}, bf16[192,896]{1,0:T(8,128)(2,1)S(1)}, u32[]{:S(2)}, u32[]{:S(2)}) collective-permute-start(bf16[192,896]{1,0:T(8,128)(2,1)} %get-tuple-element.31.refs_4_), channel_id=1, source_target_pairs={{0,2},{2,4},{4,6},{6,0},{1,3},{3,5},{5,7},{7,1},{8,10},{10,12},{12... | collective-permute-start | bytes 1032200 | tf_op jit(solution)/shard_map/ppermute | solution.py:34
  22.0 7.4 %copy-start.11 = (bf16[192,896]{1,0:T(8,128)(2,1)}, bf16[192,896]{1,0:T(8,128)(2,1)S(1)}, u32[]{:S(2)}) copy-start(bf16[192,896]{1,0:T(8,128)(2,1)S(1)} %collective-permute-done.7.refs_2_) | copy-start | bytes 1032196
  22.0 23.7 %collective-permute-start.24 = (bf16[128,1024]{1,0:T(8,128)(2,1)}, bf16[128,1024]{1,0:T(8,128)(2,1)S(1)}, u32[]{:S(2)}, u32[]{:S(2)}) collective-permute-start(bf16[128,1024]{1,0:T(8,128)(2,1)} %pad_maximum_fusion.refs_0_), channel_id=1, source_target_pairs={{0,193},{64,0},{128,64},{192,128},{1,192},{65,1},{129,65},{193,129... | collective-permute-start | bytes 786440 | tf_op jit(solution)/shard_map/ppermute | solution.py:26
  27.8 1.5 copy-start.12
  27.8 19.4 %collective-permute-start.25 = (bf16[128,1024]{1,0:T(8,128)(2,1)}, bf16[128,1024]{1,0:T(8,128)(2,1)}, u32[]{:S(2)}, u32[]{:S(2)}) collective-permute-start(bf16[128,1024]{1,0:T(8,128)(2,1)} %pad_maximum_fusion.refs_0_), channel_id=1, source_target_pairs={{0,128},{64,192},{128,1},{192,65},{1,129},{65,193},{129,0},{193,64... | collective-permute-start | bytes 786440 | tf_op jit(solution)/shard_map/ppermute | solution.py:26
  27.9 1.5 copy-start.13
  27.9 36.0 %collective-permute-start = (bf16[64,4096]{1,0:T(8,128)(2,1)}, bf16[64,4096]{1,0:T(8,128)(2,1)S(1)}, u32[]{:S(2)}, u32[]{:S(2)}) collective-permute-start(bf16[64,4096]{1,0:T(8,128)(2,1)} %get-tuple-element.24), channel_id=1, source_target_pairs={{0,193},{64,129},{128,65},{192,1},{1,192},{65,128},{129,64},{193,0... | collective-permute-start | bytes 1572872 | tf_op jit(solution)/shard_map/ppermute | solution.py:30
  29.4 0.7 copy-start.14
  30.1 0.7 copy-start.15
  34.2 39.1 %collective-permute-start.12 = (bf16[2,192,896]{2,1,0:T(8,128)(2,1)}, bf16[2,192,896]{2,1,0:T(8,128)(2,1)S(1)}, u32[]{:S(2)}, u32[]{:S(2)}) collective-permute-start(bf16[2,192,896]{2,1,0:T(8,128)(2,1)} %get-tuple-element.32.refs_0_), channel_id=1, source_target_pairs={{0,6},{2,0},{4,2},{6,4},{1,7},{3,1},{5,3},{7,5},{8,14},{10,8},{12,... | collective-permute-start | bytes 2064392 | tf_op jit(solution)/shard_map/ppermute | solution.py:34
  37.9 47.6 %copy-start = (bf16[2,192,896]{2,1,0:T(8,128)(2,1)S(1)}, bf16[2,192,896]{2,1,0:T(8,128)(2,1)}, u32[]{:S(2)}) copy-start(bf16[2,192,896]{2,1,0:T(8,128)(2,1)} %get-tuple-element.34.refs_8_) | copy-start | bytes 2064388
  37.9 38.7 %collective-permute-start.13 = (bf16[2,192,896]{2,1,0:T(8,128)(2,1)}, bf16[2,192,896]{2,1,0:T(8,128)(2,1)S(1)}, u32[]{:S(2)}, u32[]{:S(2)}) collective-permute-start(bf16[2,192,896]{2,1,0:T(8,128)(2,1)} %get-tuple-element.33.refs_1_), channel_id=1, source_target_pairs={{0,6},{2,0},{4,2},{6,4},{1,7},{3,1},{5,3},{7,5},{8,14},{10,8},{12,... | collective-permute-start | bytes 2064392 | tf_op jit(solution)/shard_map/ppermute | solution.py:34
  45.7 18.2 %copy-start.19 = (bf16[128,1024]{1,0:T(8,128)(2,1)}, bf16[128,1024]{1,0:T(8,128)(2,1)S(1)}, u32[]{:S(2)}) copy-start(bf16[128,1024]{1,0:T(8,128)(2,1)S(1)} %collective-permute-done.24.refs_1_) | copy-start | bytes 786436
  45.7 32.8 %collective-permute-start.14 = (bf16[2,192,896]{2,1,0:T(8,128)(2,1)}, bf16[2,192,896]{2,1,0:T(8,128)(2,1)S(1)}, u32[]{:S(2)}, u32[]{:S(2)}) collective-permute-start(bf16[2,192,896]{2,1,0:T(8,128)(2,1)} %get-tuple-element.32.refs_0_), channel_id=1, source_target_pairs={{0,2},{2,4},{4,6},{6,0},{1,3},{3,5},{5,7},{7,1},{8,10},{10,12},{12... | collective-permute-start | bytes 2064392 | tf_op jit(solution)/shard_map/ppermute | solution.py:34
  47.3 38.2 %collective-permute-start.15 = (bf16[2,192,896]{2,1,0:T(8,128)(2,1)}, bf16[2,192,896]{2,1,0:T(8,128)(2,1)}, u32[]{:S(2)}, u32[]{:S(2)}) collective-permute-start(bf16[2,192,896]{2,1,0:T(8,128)(2,1)} %get-tuple-element.33.refs_1_), channel_id=1, source_target_pairs={{0,2},{2,4},{4,6},{6,0},{1,3},{3,5},{5,7},{7,1},{8,10},{10,12},{12... | collective-permute-start | bytes 2064392 | tf_op jit(solution)/shard_map/ppermute | solution.py:34
  63.9 0.8 copy-start.8
  63.9 9.4 %collective-permute-start.26 = (bf16[128,1024]{1,0:T(8,128)(2,1)}, bf16[128,1024]{1,0:T(8,128)(2,1)}, u32[]{:S(2)}, u32[]{:S(2)}) collective-permute-start(bf16[128,1024]{1,0:T(8,128)(2,1)} %pad_maximum_fusion.refs_0_), channel_id=1, source_target_pairs={{0,64},{64,128},{128,192},{192,1},{1,65},{65,129},{129,193},{193,0... | collective-permute-start | bytes 786440 | tf_op jit(solution)/shard_map/ppermute | solution.py:26
  67.5 31.1 %copy-start.1 = (bf16[2,192,896]{2,1,0:T(8,128)(2,1)S(1)}, bf16[2,192,896]{2,1,0:T(8,128)(2,1)}, u32[]{:S(2)}) copy-start(bf16[2,192,896]{2,1,0:T(8,128)(2,1)} %get-tuple-element.35.refs_9_) | copy-start | bytes 2064388
  73.3 16.3 %collective-permute-start.1 = (bf16[64,4096]{1,0:T(8,128)(2,1)}, bf16[64,4096]{1,0:T(8,128)(2,1)}, u32[]{:S(2)}, u32[]{:S(2)}) collective-permute-start(bf16[64,4096]{1,0:T(8,128)(2,1)} %get-tuple-element.25), channel_id=1, source_target_pairs={{0,64},{64,128},{128,192},{192,1},{1,65},{65,129},{129,193},{193,0... | collective-permute-start | bytes 1572872 | tf_op jit(solution)/shard_map/ppermute | solution.py:26
  73.3 30.1 %copy-start.2 = (bf16[2,192,896]{2,1,0:T(8,128)(2,1)}, bf16[2,192,896]{2,1,0:T(8,128)(2,1)S(1)}, u32[]{:S(2)}) copy-start(bf16[2,192,896]{2,1,0:T(8,128)(2,1)S(1)} %collective-permute-done.12.refs_2_) | copy-start | bytes 2064388
  73.3 16.3 %collective-permute-start.2 = (bf16[64,4096]{1,0:T(8,128)(2,1)}, bf16[64,4096]{1,0:T(8,128)(2,1)}, u32[]{:S(2)}, u32[]{:S(2)}) collective-permute-start(bf16[64,4096]{1,0:T(8,128)(2,1)} %get-tuple-element.26), channel_id=1, source_target_pairs={{0,193},{64,0},{128,64},{192,128},{1,192},{65,1},{129,65},{193,129... | collective-permute-start | bytes 1572872 | tf_op jit(solution)/shard_map/ppermute | solution.py:26
  76.5 51.3 %copy-start.3 = (bf16[2,192,896]{2,1,0:T(8,128)(2,1)}, bf16[2,192,896]{2,1,0:T(8,128)(2,1)S(1)}, u32[]{:S(2)}) copy-start(bf16[2,192,896]{2,1,0:T(8,128)(2,1)S(1)} %collective-permute-done.13.refs_3_) | copy-start | bytes 2064388
  76.5 22.2 %collective-permute-start.3 = (bf16[64,4096]{1,0:T(8,128)(2,1)}, bf16[64,4096]{1,0:T(8,128)(2,1)}, u32[]{:S(2)}, u32[]{:S(2)}) collective-permute-start(bf16[64,4096]{1,0:T(8,128)(2,1)} %get-tuple-element.27), channel_id=1, source_target_pairs={{0,128},{1,129},{192,1},{193,0},{2,130},{3,131},{194,3},{195,2},{4... | collective-permute-start | bytes 1572872 | tf_op jit(solution)/shard_map/ppermute | solution.py:30
  78.5 45.1 %copy-start.4 = (bf16[2,192,896]{2,1,0:T(8,128)(2,1)}, bf16[2,192,896]{2,1,0:T(8,128)(2,1)S(1)}, u32[]{:S(2)}) copy-start(bf16[2,192,896]{2,1,0:T(8,128)(2,1)S(1)} %collective-permute-done.14.refs_4_) | copy-start | bytes 2064388
  78.5 20.2 %collective-permute-start.4 = (bf16[64,4096]{1,0:T(8,128)(2,1)}, bf16[64,4096]{1,0:T(8,128)(2,1)}, u32[]{:S(2)}, u32[]{:S(2)}) collective-permute-start(bf16[64,4096]{1,0:T(8,128)(2,1)} %get-tuple-element.28), channel_id=1, source_target_pairs={{192,64},{193,65},{0,193},{1,192},{194,66},{195,67},{2,195},{3,194... | collective-permute-start | bytes 1572872 | tf_op jit(solution)/shard_map/ppermute | solution.py:30
  85.4 24.4 %collective-permute-start.18 = (bf16[2,192,896]{2,1,0:T(8,128)(2,1)S(1)}, bf16[2,192,896]{2,1,0:T(8,128)(2,1)}, u32[]{:S(2)}, u32[]{:S(2)}) collective-permute-start(bf16[2,192,896]{2,1,0:T(8,128)(2,1)S(1)} %copy-done), channel_id=1, source_target_pairs={{0,24},{8,0},{16,8},{24,16},{1,25},{9,1},{17,9},{25,17},{2,26},{10... | collective-permute-start | bytes 2064392 | tf_op jit(solution)/shard_map/ppermute | solution.py:34
  89.6 33.9 %collective-permute-start.27 = (bf16[4,128,1024]{2,1,0:T(8,128)(2,1)}, bf16[4,128,1024]{2,1,0:T(8,128)(2,1)}, u32[]{:S(2)}, u32[]{:S(2)}) collective-permute-start(bf16[4,128,1024]{2,1,0:T(8,128)(2,1)} %stacks.4.mine), channel_id=1, source_target_pairs={{0,32},{32,0},{1,33},{33,1},{2,34},{34,2},{3,35},{35,3},{4,36},{36... | collective-permute-start | bytes 3145736 | tf_op jit(solution)/shard_map/ppermute | solution.py:38
  89.6 25.7 %collective-permute-start.20 = (bf16[2,192,896]{2,1,0:T(8,128)(2,1)S(1)}, bf16[2,192,896]{2,1,0:T(8,128)(2,1)}, u32[]{:S(2)}, u32[]{:S(2)}) collective-permute-start(bf16[2,192,896]{2,1,0:T(8,128)(2,1)S(1)} %copy-done), channel_id=1, source_target_pairs={{0,8},{8,16},{16,24},{24,0},{1,9},{9,17},{17,25},{25,1},{2,10},{10... | collective-permute-start | bytes 2064392 | tf_op jit(solution)/shard_map/ppermute | solution.py:34
  98.7 16.6 %collective-permute-start.19 = (bf16[2,192,896]{2,1,0:T(8,128)(2,1)S(1)}, bf16[2,192,896]{2,1,0:T(8,128)(2,1)}, u32[]{:S(2)}, u32[]{:S(2)}) collective-permute-start(bf16[2,192,896]{2,1,0:T(8,128)(2,1)S(1)} %copy-done.1), channel_id=1, source_target_pairs={{0,24},{8,0},{16,8},{24,16},{1,25},{9,1},{17,9},{25,17},{2,26},{10... | collective-permute-start | bytes 2064392 | tf_op jit(solution)/shard_map/ppermute | solution.py:34
  98.7 24.8 %collective-permute-start.21 = (bf16[2,192,896]{2,1,0:T(8,128)(2,1)S(1)}, bf16[2,192,896]{2,1,0:T(8,128)(2,1)}, u32[]{:S(2)}, u32[]{:S(2)}) collective-permute-start(bf16[2,192,896]{2,1,0:T(8,128)(2,1)S(1)} %copy-done.1), channel_id=1, source_target_pairs={{0,8},{8,16},{16,24},{24,0},{1,9},{9,17},{17,25},{25,1},{2,10},{10... | collective-permute-start | bytes 2064392 | tf_op jit(solution)/shard_map/ppermute | solution.py:34
  109.9 69.2 %collective-permute-start.5 = (bf16[256,4096]{1,0:T(8,128)(2,1)}, bf16[256,4096]{1,0:T(8,128)(2,1)}, u32[]{:S(2)}, u32[]{:S(2)}) collective-permute-start(bf16[256,4096]{1,0:T(8,128)(2,1)} %join.1.part), channel_id=1, source_target_pairs={{0,32},{32,0},{1,33},{33,1},{2,34},{34,2},{3,35},{35,3},{4,36},{36... | collective-permute-start | bytes 6291464 | tf_op jit(solution)/shard_map/ppermute | solution.py:38
  115.3 12.5 %collective-permute-start.32 = (bf16[256,1024]{1,0:T(8,128)(2,1)}, bf16[256,1024]{1,0:T(8,128)(2,1)}, u32[]{:S(2)}, u32[]{:S(2)}) collective-permute-start(bf16[256,1024]{1,0:T(8,128)(2,1)} %encode.1.refs_0_), channel_id=1, source_target_pairs={{0,193},{64,0},{128,64},{192,128},{1,192},{65,1},{129,65},{193,129... | collective-permute-start | bytes 1572872 | tf_op jit(solution)/shard_map/ppermute | solution.py:26
  115.3 28.4 %collective-permute-start.33 = (bf16[256,1024]{1,0:T(8,128)(2,1)}, bf16[256,1024]{1,0:T(8,128)(2,1)}, u32[]{:S(2)}, u32[]{:S(2)}) collective-permute-start(bf16[256,1024]{1,0:T(8,128)(2,1)} %encode.1.refs_0_), channel_id=1, source_target_pairs={{0,128},{64,192},{128,1},{192,65},{1,129},{65,193},{129,0},{193,64... | collective-permute-start | bytes 1572872 | tf_op jit(solution)/shard_map/ppermute | solution.py:26
  123.5 28.9 %collective-permute-start.34 = (bf16[256,1024]{1,0:T(8,128)(2,1)}, bf16[256,1024]{1,0:T(8,128)(2,1)}, u32[]{:S(2)}, u32[]{:S(2)}) collective-permute-start(bf16[256,1024]{1,0:T(8,128)(2,1)} %encode.1.refs_0_), channel_id=1, source_target_pairs={{0,64},{64,128},{128,192},{192,1},{1,65},{65,129},{129,193},{193,0... | collective-permute-start | bytes 1572872 | tf_op jit(solution)/shard_map/ppermute | solution.py:26
  123.5 33.5 %collective-permute-start.16 = (bf16[2,192,896]{2,1,0:T(8,128)(2,1)S(1)}, bf16[2,192,896]{2,1,0:T(8,128)(2,1)S(1)}, u32[]{:S(2)}, u32[]{:S(2)}) collective-permute-start(bf16[2,192,896]{2,1,0:T(8,128)(2,1)S(1)} %collective-permute-done.14.refs_4_), channel_id=1, source_target_pairs={{0,2},{2,4},{4,6},{6,0},{1,3},{3,5},{5,7},{7,1},{8,10},{10,12},{12... | collective-permute-start | bytes 2064392 | tf_op jit(solution)/shard_map/ppermute | solution.py:34
  127.8 29.4 %collective-permute-start.17 = (bf16[2,192,896]{2,1,0:T(8,128)(2,1)S(1)}, bf16[2,192,896]{2,1,0:T(8,128)(2,1)S(1)}, u32[]{:S(2)}, u32[]{:S(2)}) collective-permute-start(bf16[2,192,896]{2,1,0:T(8,128)(2,1)S(1)} %collective-permute-done.13.refs_3_), channel_id=1, source_target_pairs={{0,6},{2,0},{4,2},{6,4},{1,7},{3,1},{5,3},{7,5},{8,14},{10,8},{12,... | collective-permute-start | bytes 2064392 | tf_op jit(solution)/shard_map/ppermute | solution.py:34
  143.7 13.5 %collective-permute-start.22 = (bf16[2,192,896]{2,1,0:T(8,128)(2,1)}, bf16[2,192,896]{2,1,0:T(8,128)(2,1)S(1)}, u32[]{:S(2)}, u32[]{:S(2)}) collective-permute-start(bf16[2,192,896]{2,1,0:T(8,128)(2,1)} %collective-permute-done.20.refs_12_), channel_id=1, source_target_pairs={{0,8},{8,16},{16,24},{24,0},{1,9},{9,17},{17,25},{25,1},{2,10},{10... | collective-permute-start | bytes 2064392 | tf_op jit(solution)/shard_map/ppermute | solution.py:34
  152.4 17.7 %collective-permute-start.23 = (bf16[2,192,896]{2,1,0:T(8,128)(2,1)}, bf16[2,192,896]{2,1,0:T(8,128)(2,1)}, u32[]{:S(2)}, u32[]{:S(2)}) collective-permute-start(bf16[2,192,896]{2,1,0:T(8,128)(2,1)} %collective-permute-done.19.refs_11_), channel_id=1, source_target_pairs={{0,24},{8,0},{16,8},{24,16},{1,25},{9,1},{17,9},{25,17},{2,26},{10... | collective-permute-start | bytes 2064392 | tf_op jit(solution)/shard_map/ppermute | solution.py:34
  157.1 13.0 %copy-start.5 = (bf16[2,192,896]{2,1,0:T(8,128)(2,1)}, bf16[2,192,896]{2,1,0:T(8,128)(2,1)S(1)}, u32[]{:S(2)}) copy-start(bf16[2,192,896]{2,1,0:T(8,128)(2,1)S(1)} %collective-permute-done.16.refs_6_) | copy-start | bytes 2064388
  157.1 69.2 %collective-permute-start.35 = (bf16[4,256,1024]{2,1,0:T(8,128)(2,1)}, bf16[4,256,1024]{2,1,0:T(8,128)(2,1)}, u32[]{:S(2)}, u32[]{:S(2)}) collective-permute-start(bf16[4,256,1024]{2,1,0:T(8,128)(2,1)} %stacks.5.mine), channel_id=1, source_target_pairs={{0,32},{32,0},{1,33},{33,1},{2,34},{34,2},{3,35},{35,3},{4,36},{36... | collective-permute-start | bytes 6291464 | tf_op jit(solution)/shard_map/ppermute | solution.py:38
  157.2 12.9 %copy-start.6 = (bf16[2,192,896]{2,1,0:T(8,128)(2,1)}, bf16[2,192,896]{2,1,0:T(8,128)(2,1)S(1)}, u32[]{:S(2)}) copy-start(bf16[2,192,896]{2,1,0:T(8,128)(2,1)S(1)} %collective-permute-done.17.refs_7_) | copy-start | bytes 2064388
  157.2 12.9 %copy-start.7 = (bf16[2,192,896]{2,1,0:T(8,128)(2,1)}, bf16[2,192,896]{2,1,0:T(8,128)(2,1)S(1)}, u32[]{:S(2)}) copy-start(bf16[2,192,896]{2,1,0:T(8,128)(2,1)S(1)} %collective-permute-done.22.refs_14_) | copy-start | bytes 2064388
  174.6 19.9 %collective-permute-start.28 = (bf16[512,256]{1,0:T(8,128)(2,1)}, bf16[512,256]{1,0:T(8,128)(2,1)S(1)}, u32[]{:S(2)}, u32[]{:S(2)}) collective-permute-start(bf16[512,256]{1,0:T(8,128)(2,1)} %down_proj.1.w0), channel_id=1, source_target_pairs={{0,6},{2,0},{4,2},{6,4},{1,7},{3,1},{5,3},{7,5},{8,14},{10,8},{12,... | collective-permute-start | bytes 786440 | tf_op jit(solution)/shard_map/ppermute | solution.py:34
  177.5 17.1 %collective-permute-start.29 = (bf16[512,256]{1,0:T(8,128)(2,1)}, bf16[512,256]{1,0:T(8,128)(2,1)S(1)}, u32[]{:S(2)}, u32[]{:S(2)}) collective-permute-start(bf16[512,256]{1,0:T(8,128)(2,1)} %down_proj.1.w0), channel_id=1, source_target_pairs={{0,4},{2,6},{4,0},{6,2},{1,5},{3,7},{5,1},{7,3},{8,12},{10,14},{12... | collective-permute-start | bytes 786440 | tf_op jit(solution)/shard_map/ppermute | solution.py:34
  178.1 16.5 %collective-permute-start.30 = (bf16[512,256]{1,0:T(8,128)(2,1)}, bf16[512,256]{1,0:T(8,128)(2,1)S(1)}, u32[]{:S(2)}, u32[]{:S(2)}) collective-permute-start(bf16[512,256]{1,0:T(8,128)(2,1)} %down_proj.1.w0), channel_id=1, source_target_pairs={{0,2},{2,4},{4,6},{6,0},{1,3},{3,5},{5,7},{7,1},{8,10},{10,12},{12... | collective-permute-start | bytes 786440 | tf_op jit(solution)/shard_map/ppermute | solution.py:34
  194.6 0.7 copy-start.16
  194.6 0.8 copy-start.17
  195.4 0.7 copy-start.18
  199.2 26.3 %copy-start.20 = (s32[256]{0:T(256)S(1)}, s32[256]{0:T(256)}, u32[]{:S(2)}) copy-start(s32[256]{0:T(256)} %param.17) | copy-start | bytes 3076
  199.2 2.1 collective-permute-start.31
  219.4 16.1 %all-to-all-start.1 = ((bf16[16,16,1024]{2,1,0:T(8,128)(2,1)}), bf16[16,16,1024]{2,1,0:T(8,128)(2,1)S(1)}, u32[]{:S(2)}, u32[]{:S(2)}) async-start(bf16[16,16,1024]{2,1,0:T(8,128)(2,1)} %candidates.1), calls=%async_computation.1 | async-start | bytes 1048576 | tf_op jit(solution)/shard_map/all_to_all | solution.py:516
  235.5 0.8 copy-start.9
